TPU v7x, 512 devices: a whole 4x4x16 slice. The times are simulated.
512 devices in a mesh: src: 4 (over y), seq: 8 (over z_hi, core), head: 16 (over z_lo, x).
Axes of the slice: x: 4, y: 4, z: 16 (z_hi: 4, z_lo: 4; z = z_hi * 4 + z_lo), core: 2. Of those that a mesh axis runs over, the one named last changes fastest.
Arguments:
- enc_out: bfloat16 [32768, 4096], P(('src', 'seq'), 'head'), parts along dimension 0, may hold values from -9 to 9
- enc_gain: float32 [4096], replicated, may hold values from 0.25 to 1.75
- key_weight: bfloat16 [4096, 4096], P('seq', 'head'), may hold values from -1 to 1
- value_weight: bfloat16 [4096, 4096], P('seq', 'head'), may hold values from -0.09375 to 0.09375
- query_weight: bfloat16 [4096, 4096], P('seq', 'head'), may hold values from -2 to 2
- out_weight: bfloat16 [4096, 4096], P('head', 'seq'), may hold values from -0.09375 to 0.09375
- dec_gain: float32 [4096], replicated, may hold values from 0.25 to 1.75
- beam_state: float32 [64, 4096], P('src'), parts along dimension 0, may hold values from -7 to 7
- parents: int32 [8, 16], P('src'), parts along dimension 0, may hold values from 0 to 15
- token_embed: bfloat16 [8, 16, 4096], P('src'), parts along dimension 0, may hold values from -6 to 6
Outputs:
- final_state: float32 [64, 4096], P('src'), parts along dimension 0
- attended: float32 [64, 4096], P('src'), parts along dimension 0
There are 4 independent parts, one for each index of `src`. A program takes and returns all parts, laid end to end along the dimension named above; an argument that names none is the same for every part. Nothing has to cross between parts.
All inputs are finite; a program needn't handle non-finite values.
Results may differ from a plain program's by a relative error of at most 0.013.
The roundings to bfloat16 on the way count: a program that leaves them out, or rounds other values in their place, can miss the bound.
Values may be sent and summed in bfloat16 or wider, within the bound.
A program may use at most 64 MiB of HBM per device.

v0:
```python
import jax
import jax.numpy as jnp
from jax import lax
from jax.sharding import PartitionSpec as P

HEAD_DIM = 64
BEAMS = 16
STEPS = 2


def rms_norm(values, gain):
    mean_square = jnp.mean(values * values, axis=-1, keepdims=True)
    return values * lax.rsqrt(mean_square + 1e-06) * gain


def on_device(
    enc_out,
    enc_gain,
    key_weight,
    value_weight,
    query_weight,
    out_weight,
    dec_gain,
    beam_state,
    parents,
    token_embed,
):
    full_rows = lax.all_gather(enc_out, "head", axis=1, tiled=True)
    memory = rms_norm(full_rows.astype(jnp.float32), enc_gain).astype(jnp.bfloat16)
    key_full, value_full = (
        lax.all_gather(key_weight, "seq", axis=0, tiled=True),
        lax.all_gather(value_weight, "seq", axis=0, tiled=True),
    )
    rows = memory.shape[0]
    heads_here = key_weight.shape[1] // HEAD_DIM
    keys = jnp.dot(memory, key_full, preferred_element_type=jnp.float32).astype(jnp.bfloat16)
    values = jnp.dot(memory, value_full, preferred_element_type=jnp.float32).astype(jnp.bfloat16)
    keys = keys.reshape(rows, heads_here, HEAD_DIM)
    values = values.reshape(rows, heads_here, HEAD_DIM)
    feat_rows = query_weight.shape[0]
    feat_start = lax.axis_index("seq") * feat_rows
    state = beam_state
    attended = jnp.zeros(beam_state.shape, jnp.float32)
    for step in range(STEPS):
        state = jnp.take(state, parents[step], axis=0) + token_embed[step].astype(jnp.float32)
        normed = rms_norm(state, dec_gain).astype(jnp.bfloat16)
        normed_part = lax.dynamic_slice_in_dim(normed, feat_start, feat_rows, 1)
        query_part = jnp.dot(normed_part, query_weight, preferred_element_type=jnp.float32)
        query = lax.psum(query_part, "seq").astype(jnp.bfloat16)
        query = query.reshape(BEAMS, heads_here, HEAD_DIM)
        scores = jnp.einsum("bhd,shd->bhs", query, keys, preferred_element_type=jnp.float32) * 0.125
        top = jnp.max(scores, axis=-1)
        expo = jnp.exp(scores - top[..., None])
        total = jnp.sum(expo, axis=-1)
        weights = expo.astype(jnp.bfloat16)
        weighted = jnp.einsum("bhs,shd->bhd", weights, values, preferred_element_type=jnp.float32)
        peak_all = lax.pmax(top, "seq")
        factor = jnp.exp(top - peak_all)
        total_all, weighted_all = lax.psum((total * factor, weighted * factor[..., None]), "seq")
        context = (weighted_all / total_all[..., None]).astype(jnp.bfloat16)
        context = context.reshape(BEAMS, heads_here * HEAD_DIM)
        partial_out = jnp.dot(context, out_weight, preferred_element_type=jnp.float32)
        columns = lax.psum(partial_out.astype(jnp.bfloat16), "head").astype(jnp.float32)
        added = lax.all_gather(columns.astype(jnp.bfloat16), "seq", axis=1, tiled=True).astype(
            columns.dtype
        )
        state = state + added
        attended = attended + added
    return (state, attended)


def solution(mesh):
    placed = (
        P(("src", "seq"), "head"),
        P(),
        P("seq", "head"),
        P("seq", "head"),
        P("seq", "head"),
        P("head", "seq"),
        P(),
        P("src", None),
        P("src", None),
        P("src", None, None),
    )
    return jax.shard_map(
        on_device,
        mesh=mesh,
        in_specs=placed,
        out_specs=(P("src", None), P("src", None)),
        check_vma=False,
    )
```

profile of v0, /device:TPU:6, one launch (start us, length us, event | category | flops | bytes accessed | tf_op | source)
XLA Modules:
  0.0 592.7 jit_solution(18296726417365405977)
XLA Ops:
  7.2 0.7 all-gather.4.cloned.1.call-update
  8.0 0.7 all-gather.8.cloned.1.call-update
  8.7 0.7 all-gather.6.cloned.1.call-update
  9.4 0.8 compare_and_fusion
  10.2 0.6 gather_fusion
  10.8 0.8 dynamic-slice
  11.6 1.1 multiply_reduce_fusion.1
  12.7 1.1 fusion.29
  13.9 45.7 %psum.56 = bf16[16,256]{1,0:T(8,128)(2,1)S(1)} all-reduce(f32[16,256]{1,0:T(8,128)S(1)} %fusion.29), channel_id=1, replica_groups=mesh['src'=4,'seq'=8,'head'=16] {'seq'}, use_global_device_ids=true, to_apply=%region_2.4 | all-reduce | flops 4096 | bytes 24576 | tf_op jit(solution)/shard_map/psum | solution.py:49
  59.7 85.0 %all-gather.4.cloned.1.call-done = bf16[1024,4096]{1,0:T(8,128)(2,1)} async-done(((bf16[1024,256]{1,0:T(8,128)(2,1)}), bf16[1024,4096]{1,0:T(8,128)(2,1)}) %all-gather.4.cloned.1.call-update) | async-done | bytes 8388624 | tf_op jit(solution)/shard_map/all_gather | solution.py:28
  144.7 5.1 fusion
  149.8 58.4 %all-gather.8.cloned.1.call-done = bf16[4096,256]{1,0:T(8,128)(2,1)} async-done(((bf16[512,256]{1,0:T(8,128)(2,1)}), bf16[4096,256]{1,0:T(8,128)(2,1)}) %all-gather.8.cloned.1.call-update) | async-done | bytes 2097168 | tf_op jit(solution)/shard_map/all_gather | solution.py:31
  208.2 6.6 %fusion.10 = bf16[1024,256]{0,1:T(8,128)(2,1)S(1)} fusion(bf16[4096,256]{1,0:T(8,128)(2,1)} %all-gather.8.cloned.1.call-done, bf16[1024,4096]{1,0:T(8,128)(2,1)} %all-gather.4.cloned.1.call-done, f32[4096]{0:T(1024)S(1)} %copy-done.4, f32[1024]{0:T(1024)S(1)} %add_rsqrt_fusion), kind=kOutput, calls=%fused_computation.10 | convolution fusion | flops 2164523008 | bytes 11030528 | tf_op jit(solution)/shard_map/dot_general | solution.py:36
  214.9 0.3 fusion.43
  215.1 21.7 %pmax.14 = f32[16,4]{0,1:T(4,128)S(1)} all-reduce(f32[16,4]{0,1:T(4,128)S(1)} %get-tuple-element.23), channel_id=1, replica_groups=mesh['src'=4,'seq'=8,'head'=16] {'seq'}, use_global_device_ids=true, to_apply=%region_4.6 | all-reduce | flops 64 | bytes 512 | tf_op jit(solution)/shard_map/pmax | solution.py:57
  237.1 28.6 %all-gather.6.cloned.1.call-done = bf16[4096,256]{1,0:T(8,128)(2,1)} async-done(((bf16[512,256]{1,0:T(8,128)(2,1)}), bf16[4096,256]{1,0:T(8,128)(2,1)}) %all-gather.6.cloned.1.call-update) | async-done | bytes 2097168 | tf_op jit(solution)/shard_map/all_gather | solution.py:32
  265.6 6.6 %fusion.7 = bf16[1024,256]{0,1:T(8,128)(2,1)S(1)} fusion(bf16[4096,256]{1,0:T(8,128)(2,1)} %all-gather.6.cloned.1.call-done, bf16[1024,4096]{1,0:T(8,128)(2,1)} %all-gather.4.cloned.1.call-done, f32[4096]{0:T(1024)S(1)} %copy-done.4, f32[1024]{0:T(1024)S(1)} %add_rsqrt_fusion), kind=kOutput, calls=%fused_computation.9 | convolution fusion | flops 2164523008 | bytes 11030528 | tf_op jit(solution)/shard_map/dot_general | solution.py:37
  272.3 0.3 fusion.16
  272.5 38.8 %all-reduce.1 = (f32[16,4,64]{2,0,1:T(8,128)S(1)}, f32[16,4]{0,1:T(4,128)S(1)}) all-reduce(f32[16,4,64]{2,0,1:T(8,128)S(1)} %fusion.16, f32[16,4]{0,1:T(4,128)S(1)} %get-tuple-element.13), channel_id=1, replica_groups=mesh['src'=4,'seq'=8,'head'=16] {'seq'}, use_global_device_ids=true, to_apply=%region_5.7 | all-reduce | flops 4160 | bytes 33280 | tf_op jit(solution)/shard_map/psum | solution.py:59
  311.7 66.3 %psum.59 = bf16[16,512]{1,0:T(8,128)(2,1)S(1)} all-reduce(bf16[16,512]{1,0:T(8,128)(2,1)S(1)} %convolution_convert_fusion.1), channel_id=1, replica_groups=mesh['src'=4,'seq'=8,'head'=16] {'head'}, use_global_device_ids=true, to_apply=%region_8.10 | all-reduce | flops 8192 | bytes 32768 | tf_op jit(solution)/shard_map/psum | solution.py:63
  378.1 18.3 %all_gather.18 = bf16[16,4096]{1,0:T(8,128)(2,1)S(1)} all-gather(bf16[16,512]{1,0:T(8,128)(2,1)S(1)} %psum.59), channel_id=1, replica_groups=mesh['src'=4,'seq'=8,'head'=16] {'seq'}, dimensions={1}, use_global_device_ids=true | all-gather | bytes 147456 | tf_op jit(solution)/shard_map/all_gather | solution.py:64
  396.4 0.6 gather_fusion.1
  397.0 0.2 multiply_reduce_fusion
  397.3 0.2 fusion.31
  397.5 38.8 %psum.60 = bf16[16,256]{1,0:T(8,128)(2,1)S(1)} all-reduce(f32[16,256]{1,0:T(8,128)S(1)} %fusion.31), channel_id=1, replica_groups=mesh['src'=4,'seq'=8,'head'=16] {'seq'}, use_global_device_ids=true, to_apply=%region_10.12 | all-reduce | flops 4096 | bytes 24576 | tf_op jit(solution)/shard_map/psum | solution.py:49
  436.4 0.3 fusion.44
  436.7 17.8 %pmax.15 = f32[16,4]{0,1:T(4,128)S(1)} all-reduce(f32[16,4]{0,1:T(4,128)S(1)} %get-tuple-element.25), channel_id=1, replica_groups=mesh['src'=4,'seq'=8,'head'=16] {'seq'}, use_global_device_ids=true, to_apply=%region_12.14 | all-reduce | flops 64 | bytes 512 | tf_op jit(solution)/shard_map/pmax | solution.py:57
  454.7 0.3 fusion.15
  455.0 35.7 %all-reduce = (f32[16,4,64]{2,0,1:T(8,128)S(1)}, f32[16,4]{0,1:T(4,128)S(1)}) all-reduce(f32[16,4,64]{2,0,1:T(8,128)S(1)} %fusion.15, f32[16,4]{0,1:T(4,128)S(1)} %get-tuple-element.7), channel_id=1, replica_groups=mesh['src'=4,'seq'=8,'head'=16] {'seq'}, use_global_device_ids=true, to_apply=%region_13.15 | all-reduce | flops 4160 | bytes 33280 | tf_op jit(solution)/shard_map/psum | solution.py:59
  491.0 75.9 %psum.63 = bf16[16,512]{1,0:T(8,128)(2,1)S(1)} all-reduce(bf16[16,512]{1,0:T(8,128)(2,1)S(1)} %convolution_convert_fusion), channel_id=1, replica_groups=mesh['src'=4,'seq'=8,'head'=16] {'head'}, use_global_device_ids=true, to_apply=%region_16.18 | all-reduce | flops 8192 | bytes 32768 | tf_op jit(solution)/shard_map/psum | solution.py:63
  566.9 18.5 %all_gather.19 = bf16[16,4096]{1,0:T(8,128)(2,1)S(1)} all-gather(bf16[16,512]{1,0:T(8,128)(2,1)S(1)} %psum.63), channel_id=1, replica_groups=mesh['src'=4,'seq'=8,'head'=16] {'seq'}, dimensions={1}, use_global_device_ids=true | all-gather | bytes 147456 | tf_op jit(solution)/shard_map/all_gather | solution.py:64
  585.4 0.8 convert_add_fusion
  (33 shorter events, 1.4 us)
Async XLA Ops:
  7.2 3.0 copy-start
  7.2 201.1 %copy-start.4 = (f32[4096]{0:T(1024)S(1)}, f32[4096]{0:T(1024)}, u32[]{:S(2)}) copy-start(f32[4096]{0:T(1024)} %param.13) | copy-start | bytes 49156
  7.2 137.5 %all-gather.4.cloned.1.call-start = ((), (), s32[]{:S(2)}) async-start(), calls=%async_computation | async-start | bytes 8912896 | tf_op jit(solution)/shard_map/all_gather | solution.py:28
  7.9 200.3 %all-gather.8.cloned.1.call-start = ((), (), s32[]{:S(2)}) async-start(), calls=%async_computation.2 | async-start | bytes 2359296 | tf_op jit(solution)/shard_map/all_gather | solution.py:31
  8.7 257.0 %all-gather.6.cloned.1.call-start = ((), (), s32[]{:S(2)}) async-start(), calls=%async_computation.1 | async-start | bytes 2359296 | tf_op jit(solution)/shard_map/all_gather | solution.py:32
  237.0 74.6 %copy-start.2 = (bf16[256,512]{1,0:T(8,128)(2,1)S(1)}, bf16[256,512]{1,0:T(8,128)(2,1)}, u32[]{:S(2)}) copy-start(bf16[256,512]{1,0:T(8,128)(2,1)} %param.17) | copy-start | bytes 786436
  237.0 160.0 %copy-start.3 = (bf16[2,16,4096]{2,1,0:T(8,128)(2,1)S(1)}, bf16[2,16,4096]{2,1,0:T(8,128)(2,1)}, u32[]{:S(2)}) copy-start(bf16[2,16,4096]{2,1,0:T(8,128)(2,1)} %param.21) | copy-start | bytes 786436
  237.0 160.2 %copy-start.1 = (bf16[512,256]{1,0:T(8,128)(2,1)S(1)}, bf16[512,256]{1,0:T(8,128)(2,1)}, u32[]{:S(2)}) copy-start(bf16[512,256]{1,0:T(8,128)(2,1)} %param.16) | copy-start | bytes 786436
Sparse Core Ops, SparseCore 0:
  10.0 134.6 all-gather.3
  146.9 61.3 all-gather.7
  210.4 55.1 all-gather.5
where the time goes:
time: 603 us; the launch traced here: 593 us
  blocking collectives  378 us (63%)
  waiting for transfers between devices  174 us (29%)
  matrix products  15.9 us (3%)
  between operations  13.9 us (2%)
  other arithmetic  8.64 us (1%)
    psum x2, blocking collectives, on_device(): lax.psum(partial_out.astype(jnp.bfloat16), 'head').astype(jnp.float32)  142 us
    all_gather x1, waiting for transfers between devices, on_device(): full_rows = lax.all_gather(enc_out, 'head', axis=1, tiled=True)  85 us
    psum x2, blocking collectives, on_device(): query = lax.psum(query_part, 'seq').astype(jnp.bfloat16)  84.5 us
    psum x2, blocking collectives, on_device(): lax.psum((total * factor, weighted * factor[..., None]), 'seq')  74.6 us
    all_gather x1, waiting for transfers between devices, on_device(): lax.all_gather(key_weight, 'seq', axis=0, tiled=True)  58.4 us
    pmax x2, blocking collectives, on_device(): peak_all = lax.pmax(top, 'seq')  39.5 us
    all_gather x2, blocking collectives, on_device(): lax.all_gather(columns.astype(jnp.bfloat16), 'seq', axis=1, tiled=True)  36.8 us
    all_gather x1, waiting for transfers between devices, on_device(): lax.all_gather(value_weight, 'seq', axis=0, tiled=True)  28.6 us
  transfers between devices with their start and end apart: 3, of which 3 were waited for; matrix products, arithmetic and copies ran while one was open for 3% of the time, Pallas kernels for 0%

commit v1 on v0

v1 whole, which is shorter than its diff:
```python
import functools

import jax
import jax.numpy as jnp
from jax import lax
from jax.experimental import pallas as pl
from jax.experimental.pallas import tpu as pltpu
from jax.sharding import PartitionSpec as P

MESH = pl.DeviceIdType.MESH
HEAD_DIM = 64
BEAMS = 16
STEPS = 2
SEQ = 8
HEAD = 16


def rms_norm(values, gain):
    mean_square = jnp.mean(values * values, axis=-1, keepdims=True)
    return values * lax.rsqrt(mean_square + 1e-06) * gain


def decode_kernel(
    keys, vals, wq, wo, gain, first, parents, tokens,
    out_state, out_att,
    state, nrm, q_own, q_all, c_own, c_all, t_own, t_all, p_own, p_all, f_own, f_all, g_all,
    q_ss, q_rs, c_ss, c_rs, t_ss, t_rs, p_ss, p_rs, f_ss, f_rs, g_ss, g_rs,
):
    s = lax.axis_index("seq")
    c = lax.axis_index("head")
    seq_peers = [lax.rem(s + k, SEQ) for k in range(1, SEQ)]
    head_peers = [lax.rem(c + k, HEAD) for k in range(1, HEAD)]

    barrier = pltpu.get_barrier_semaphore()
    for p in seq_peers:
        pl.semaphore_signal(barrier, inc=1, device_id={"seq": p}, device_id_type=MESH)
    for p in head_peers:
        pl.semaphore_signal(barrier, inc=1, device_id={"head": p}, device_id_type=MESH)
    pl.semaphore_wait(barrier, SEQ + HEAD - 2)

    sent = []

    def send(src, dst, ss, rs, where):
        copy = pltpu.make_async_remote_copy(
            src_ref=src, dst_ref=dst, send_sem=ss, recv_sem=rs,
            device_id=where, device_id_type=MESH,
        )
        copy.start()
        sent.append(copy)

    def arrived(dst, rs, ss, where):
        pltpu.make_async_remote_copy(
            src_ref=dst, dst_ref=dst, send_sem=ss, recv_sem=rs,
            device_id=where, device_id_type=MESH,
        ).wait_recv()

    col_head = lax.broadcasted_iota(jnp.int32, (BEAMS, 256), 1) // HEAD_DIM
    lane = lax.broadcasted_iota(jnp.int32, (8, 128), 1)

    for t in range(STEPS):
        for b in range(BEAMS):
            source = first[parents[t, b]] if t == 0 else state[t - 1, parents[t, b]]
            row = source + tokens[t, b]
            square = jnp.sum(jnp.sum(row * row, axis=0), axis=(0, 1), keepdims=True) * (1.0 / 4096.0)
            state[t, b] = row
            nrm[b] = row * lax.rsqrt(square + 1e-06)[None] * gain[...]
        part = jnp.zeros((BEAMS, 256), jnp.float32)
        for j in range(4):
            part += jnp.dot(
                nrm[:, s, j, :].astype(jnp.bfloat16), wq[pl.ds(128 * j, 128), :],
                preferred_element_type=jnp.float32,
            )
        q_own[t] = part
        q_all[t, s] = part
        for k, p in enumerate(seq_peers):
            send(q_own.at[t], q_all.at[t, s], q_ss.at[t, k], q_rs.at[t, s], {"seq": p})
        for k, p in enumerate(seq_peers):
            arrived(q_all.at[t, p], q_rs.at[t, p], q_ss.at[t, k], {"seq": p})
        query = q_all[t, 0]
        for i in range(1, SEQ):
            query += q_all[t, i]
        query = query.astype(jnp.bfloat16).astype(jnp.float32)
        spread = jnp.concatenate(
            [jnp.where(col_head == h, query, 0.0) for h in range(4)], axis=0
        ).astype(jnp.bfloat16)
        scores = lax.dot_general(
            spread, keys[...], (((1,), (1,)), ((), ())), preferred_element_type=jnp.float32
        ) * 0.125
        top = jnp.max(scores, axis=-1, keepdims=True)
        expo = jnp.exp(scores - top)
        total = jnp.sum(expo, axis=-1, keepdims=True)
        mixed = jnp.dot(expo.astype(jnp.bfloat16), vals[...], preferred_element_type=jnp.float32)
        ctx = jnp.zeros((BEAMS, 256), jnp.float32)
        stats = jnp.zeros((8, 128), jnp.float32)
        for h in range(4):
            ctx += jnp.where(col_head == h, mixed[16 * h:16 * h + 16], 0.0)
            for half in range(2):
                at = 16 * h + 8 * half
                stats = jnp.where(lane == 8 * half + h, top[at:at + 8], stats)
                stats = jnp.where(lane == 8 * half + 4 + h, total[at:at + 8], stats)
        ctx = ctx.astype(jnp.bfloat16)
        c_own[t] = ctx
        t_own[t] = stats
        c_all[t, s] = ctx
        t_all[t, s] = stats
        for k, p in enumerate(seq_peers):
            send(t_own.at[t], t_all.at[t, s], t_ss.at[t, k], t_rs.at[t, s], {"seq": p})
            send(c_own.at[t], c_all.at[t, s], c_ss.at[t, k], c_rs.at[t, s], {"seq": p})
        for k, p in enumerate(seq_peers):
            arrived(t_all.at[t, p], t_rs.at[t, p], t_ss.at[t, k], {"seq": p})
            arrived(c_all.at[t, p], c_rs.at[t, p], c_ss.at[t, k], {"seq": p})
        each = [t_all[t, i] for i in range(SEQ)]
        peak = functools.reduce(jnp.maximum, each)
        factors = [jnp.exp(one - peak) for one in each]
        sums = functools.reduce(
            lambda a, b: a + b, [f * pltpu.roll(one, 124, 1) for f, one in zip(factors, each)]
        )
        halves = []
        for half in range(2):
            acc = jnp.zeros((8, 256), jnp.float32)
            for i in range(SEQ):
                share = factors[i] / sums
                scale = jnp.zeros((8, 256), jnp.float32)
                for h in range(4):
                    at = 8 * half + h
                    scale = jnp.where(
                        col_head[:8] == h, jnp.broadcast_to(share[:, at:at + 1], (8, 256)), scale
                    )
                acc += c_all[t, i].astype(jnp.float32)[8 * half:8 * half + 8] * scale
            halves.append(acc)
        context = jnp.concatenate(halves, axis=0).astype(jnp.bfloat16)
        partial = jnp.dot(context, wo[...], preferred_element_type=jnp.float32)
        for j in range(4):
            p_own[t, :, j, :] = partial[:, 128 * j:128 * j + 128]
        p_all[t, c] = p_own[t, c]
        for k, p in enumerate(head_peers):
            send(p_own.at[t, p], p_all.at[t, c], p_ss.at[t, k], p_rs.at[t, c], {"head": p})
        for k, p in enumerate(head_peers):
            arrived(p_all.at[t, p], p_rs.at[t, p], p_ss.at[t, k], {"head": p})
        row = p_all[t, 0]
        for i in range(1, HEAD):
            row += p_all[t, i]
        f_own[t] = row
        f_all[t, s] = row
        for k, p in enumerate(seq_peers):
            send(f_own.at[t], f_all.at[t, s], f_ss.at[t, k], f_rs.at[t, s], {"seq": p})
        for k, p in enumerate(seq_peers):
            arrived(f_all.at[t, p], f_rs.at[t, p], f_ss.at[t, k], {"seq": p})
        for k, p in enumerate(head_peers):
            send(f_all.at[t], g_all.at[t, c], g_ss.at[t, k], g_rs.at[t, c], {"head": p})
        g_all[t, c] = f_all[t]
        for k, p in enumerate(head_peers):
            arrived(g_all.at[t, p], g_rs.at[t, p], g_ss.at[t, k], {"head": p})
        for b in range(BEAMS):
            state[t, b] = state[t, b] + g_all[t, b]
    for b in range(BEAMS):
        out_state[b] = state[STEPS - 1, b]
        out_att[b] = g_all[0, b] + g_all[1, b]
    for copy in sent:
        copy.wait_send()


def decode(keys, values, wq, wo, gain, first, parents, tokens):
    vmem = pl.BlockSpec(memory_space=pltpu.VMEM)
    f32, bf16 = jnp.float32, jnp.bfloat16
    dma = pltpu.SemaphoreType.DMA
    rows = jax.ShapeDtypeStruct((BEAMS, 8, 4, 128), f32)
    return pl.pallas_call(
        decode_kernel,
        out_shape=(rows, rows),
        in_specs=[vmem] * 6 + [pl.BlockSpec(memory_space=pltpu.SMEM), vmem],
        out_specs=(vmem, vmem),
        scratch_shapes=[
            pltpu.VMEM((STEPS, BEAMS, 8, 4, 128), f32),
            pltpu.VMEM((BEAMS, 8, 4, 128), f32),
            pltpu.VMEM((STEPS, BEAMS, 256), f32),
            pltpu.VMEM((STEPS, SEQ, BEAMS, 256), f32),
            pltpu.VMEM((STEPS, BEAMS, 256), bf16),
            pltpu.VMEM((STEPS, SEQ, BEAMS, 256), bf16),
            pltpu.VMEM((STEPS, 8, 128), f32),
            pltpu.VMEM((STEPS, SEQ, 8, 128), f32),
            pltpu.VMEM((STEPS, BEAMS, 4, 128), f32),
            pltpu.VMEM((STEPS, HEAD, 4, 128), f32),
            pltpu.VMEM((STEPS, 4, 128), f32),
            pltpu.VMEM((STEPS, SEQ, 4, 128), f32),
            pltpu.VMEM((STEPS, BEAMS, 8, 4, 128), f32),
            dma((STEPS, SEQ)), dma((STEPS, SEQ)),
            dma((STEPS, SEQ)), dma((STEPS, SEQ)),
            dma((STEPS, SEQ)), dma((STEPS, SEQ)),
            dma((STEPS, HEAD)), dma((STEPS, HEAD)),
            dma((STEPS, SEQ)), dma((STEPS, SEQ)),
            dma((STEPS, HEAD)), dma((STEPS, HEAD)),
        ],
        compiler_params=pltpu.CompilerParams(collective_id=1, has_side_effects=True),
        name="decode",
    )(keys, values, wq, wo, gain, first, parents, tokens)


def on_device(
    enc_out, enc_gain, key_weight, value_weight, query_weight, out_weight,
    dec_gain, beam_state, parents, token_embed,
):
    full_rows = lax.all_gather(enc_out, "head", axis=1, tiled=True)
    memory = rms_norm(full_rows.astype(jnp.float32), enc_gain).astype(jnp.bfloat16)
    key_full = lax.all_gather(key_weight, "seq", axis=0, tiled=True)
    value_full = lax.all_gather(value_weight, "seq", axis=0, tiled=True)
    keys = jnp.dot(memory, key_full, preferred_element_type=jnp.float32).astype(jnp.bfloat16)
    values = jnp.dot(memory, value_full, preferred_element_type=jnp.float32).astype(jnp.bfloat16)
    state, attended = decode(
        keys, values, query_weight, out_weight,
        dec_gain.reshape(8, 4, 128),
        beam_state.reshape(BEAMS, 8, 4, 128),
        parents,
        token_embed.astype(jnp.float32).reshape(STEPS, BEAMS, 8, 4, 128),
    )
    return state.reshape(BEAMS, 4096), attended.reshape(BEAMS, 4096)


def solution(mesh):
    placed = (
        P(("src", "seq"), "head"),
        P(),
        P("seq", "head"),
        P("seq", "head"),
        P("seq", "head"),
        P("head", "seq"),
        P(),
        P("src", None),
        P("src", None),
        P("src", None, None),
    )
    return jax.shard_map(
        on_device,
        mesh=mesh,
        in_specs=placed,
        out_specs=(P("src", None), P("src", None)),
        check_vma=False,
    )
```

time: 603 us -> 373 us (0.62); the launches traced: 593 us -> 373 us
  blocking collectives: 378 us -> 0 us
  Pallas kernels: 0 us -> 90.5 us
  waiting for transfers between devices: 174 us -> 241 us
    psum x6 -> x0, blocking collectives: 301 us -> none  [the longest x2 142 us: on_device(): lax.psum(partial_out.astype(jnp.bfloat16), 'head').astype(jnp.float32)]
    pallas_call x0 -> x1, Pallas kernels: none -> 90.5 us  [decode(): pl.pallas_call(decode_kernel, out_shape=(rows, rows), in_specs=[vmem] * 6...]
    all_gather x1, waiting for transfers between devices: 85 us -> 130 us  [on_device(): full_rows = lax.all_gather(enc_out, 'head', axis=1, tiled=True)]
    pmax x2 -> x0, blocking collectives: 39.5 us -> none  [on_device(): peak_all = lax.pmax(top, 'seq')]
    all_gather x2 -> x0, blocking collectives: 36.8 us -> none  [on_device(): lax.all_gather(columns.astype(jnp.bfloat16), 'seq', axis=1, tiled=True)]
    all_gather x2, waiting for transfers between devices: 87 us -> 110 us  [the longest x1 58.3 us: on_device(): value_full = lax.all_gather(value_weight, 'seq', axis=0, tiled=True)]
    reshape x4, local copies, waits for them, and re-layouts: 0.36 us -> 7.55 us  [the longest x2 3.52 us: on_device(): return (state.reshape(BEAMS, 4096), attended.reshape(BEAMS, 4096))]
  transfers between devices with their start and end apart: 3 -> 3, of which waited for: 3 -> 3; matrix products, arithmetic and copies ran while one was open for 3% -> 4% of each run, Pallas kernels for 0% -> 0%
where the time goes in v1:
time: 373 us
  waiting for transfers between devices  241 us (65%)
  Pallas kernels  90.5 us (24%)
  matrix products  14.4 us (4%)
  between operations  13.8 us (4%)
  local copies, waits for them, and re-layouts  7.56 us (2%)
  other arithmetic  5.08 us (1%)
    all_gather x1, waiting for transfers between devices, on_device(): full_rows = lax.all_gather(enc_out, 'head', axis=1, tiled=True)  130 us
    pallas_call x1, Pallas kernels, decode(): pl.pallas_call(decode_kernel, out_shape=(rows, rows), in_specs=[vmem] * 6...  90.5 us
    all_gather x1, waiting for transfers between devices, on_device(): value_full = lax.all_gather(value_weight, 'seq', axis=0, tiled=True)  58.3 us
    all_gather x1, waiting for transfers between devices, on_device(): key_full = lax.all_gather(key_weight, 'seq', axis=0, tiled=True)  51.4 us
  transfers between devices with their start and end apart: 3, of which 3 were waited for; matrix products, arithmetic and copies ran while one was open for 4% of the time, Pallas kernels for 0%

profile of v1, /device:TPU:6, one launch (start us, length us, event | category | flops | bytes accessed | tf_op | source)
XLA Modules:
  0.0 372.8 jit_solution(14469319453654028624)
XLA Ops:
  7.2 0.0 copy-start
  7.2 0.0 all-gather.4.cloned.1.call-start
  7.2 0.7 all-gather.4.cloned.1.call-update
  7.9 0.0 all-gather.8.cloned.1.call-start
  8.0 0.7 all-gather.8.cloned.1.call-update
  8.7 0.0 all-gather.6.cloned.1.call-start
  8.7 0.7 all-gather.6.cloned.1.call-update
  9.4 2.2 reshape.37.tokens
  11.6 1.8 reshape.31.first
  13.4 129.6 %all-gather.4.cloned.1.call-done = bf16[1024,4096]{1,0:T(8,128)(2,1)} async-done(((bf16[1024,256]{1,0:T(8,128)(2,1)}), bf16[1024,4096]{1,0:T(8,128)(2,1)}) %all-gather.4.cloned.1.call-update) | async-done | bytes 8388624 | tf_op jit(solution)/shard_map/all_gather | solution.py:203
  143.0 5.1 %fusion = f32[1024]{0:T(1024)S(1)} fusion(bf16[1024,4096]{1,0:T(8,128)(2,1)} %all-gather.4.cloned.1.call-done), kind=kLoop, calls=%fused_computation.2 | loop fusion | flops 12581888 | bytes 8392704 | tf_op jit(solution)/shard_map/reduce_sum | solution.py:19
  148.1 58.3 %all-gather.8.cloned.1.call-done = bf16[4096,256]{1,0:T(8,128)(2,1)} async-done(((bf16[512,256]{1,0:T(8,128)(2,1)}), bf16[4096,256]{1,0:T(8,128)(2,1)}) %all-gather.8.cloned.1.call-update) | async-done | bytes 2097168 | tf_op jit(solution)/shard_map/all_gather | solution.py:206
  206.4 0.0 copy-done
  206.4 7.2 %fusion.10.vals = bf16[1024,256]{1,0:T(8,128)(2,1)} fusion(bf16[4096,256]{1,0:T(8,128)(2,1)} %all-gather.8.cloned.1.call-done, bf16[1024,4096]{1,0:T(8,128)(2,1)} %all-gather.4.cloned.1.call-done, f32[4096]{0:T(1024)S(1)} %copy-done, f32[1024]{0:T(1024)S(1)} %add_rsqrt_fusion), kind=kOutput, calls=%fused_computation.8 | convolution fusion | flops 2164523008 | bytes 11030528 | tf_op jit(solution)/shard_map/dot_general | solution.py:208
  213.6 51.4 %all-gather.6.cloned.1.call-done = bf16[4096,256]{1,0:T(8,128)(2,1)} async-done(((bf16[512,256]{1,0:T(8,128)(2,1)}), bf16[4096,256]{1,0:T(8,128)(2,1)}) %all-gather.6.cloned.1.call-update) | async-done | bytes 2097168 | tf_op jit(solution)/shard_map/all_gather | solution.py:205
  265.0 7.2 %fusion.7.keys = bf16[1024,256]{1,0:T(8,128)(2,1)} fusion(bf16[4096,256]{1,0:T(8,128)(2,1)} %all-gather.6.cloned.1.call-done, bf16[1024,4096]{1,0:T(8,128)(2,1)} %all-gather.4.cloned.1.call-done, f32[4096]{0:T(1024)S(1)} %copy-done, f32[1024]{0:T(1024)S(1)} %add_rsqrt_fusion), kind=kOutput, calls=%fused_computation.7 | convolution fusion | flops 2164523008 | bytes 11030528 | tf_op jit(solution)/shard_map/dot_general | solution.py:207
  272.2 90.5 %decode.1 = (f32[16,8,4,128]{3,2,1,0:T(4,128)}, f32[16,8,4,128]{3,2,1,0:T(4,128)}) custom-call(bf16[1024,256]{1,0:T(8,128)(2,1)} %fusion.7.keys, bf16[1024,256]{1,0:T(8,128)(2,1)} %fusion.10.vals, bf16[512,256]{1,0:T(8,128)(2,1)} %wq.1, bf16[256,512]{1,0:T(8,128)(2,1)} %wo.1, f32[8,4,128]{2,1,0:T(4,128)} %bitcast.3, f32[16,8,4,128]{3,2,1,0:T(4,128)} %reshape.31.first, ...), custom_call_target="tpu_custom_call" | custom-call | tf_op jit(solution)/shard_map/decode/pallas_call | solution.py:168
  362.7 1.8 reshape.34
  364.5 1.8 reshape.35
  (1 shorter events, 0.0 us)
Async XLA Ops:
  7.2 199.2 %copy-start = (f32[4096]{0:T(1024)S(1)}, f32[4096]{0:T(1024)}, u32[]{:S(2)}) copy-start(f32[4096]{0:T(1024)} %param.11) | copy-start | bytes 49156
  7.2 135.8 %all-gather.4.cloned.1.call-start = ((), (), s32[]{:S(2)}) async-start(), calls=%async_computation | async-start | bytes 8912896 | tf_op jit(solution)/shard_map/all_gather | solution.py:203
  7.9 198.5 %all-gather.8.cloned.1.call-start = ((), (), s32[]{:S(2)}) async-start(), calls=%async_computation.2 | async-start | bytes 2359296 | tf_op jit(solution)/shard_map/all_gather | solution.py:206
  8.7 256.4 %all-gather.6.cloned.1.call-start = ((), (), s32[]{:S(2)}) async-start(), calls=%async_computation.1 | async-start | bytes 2359296 | tf_op jit(solution)/shard_map/all_gather | solution.py:205
Sparse Core Ops, SparseCore 0:
  10.0 132.9 all-gather.3
  145.1 61.2 all-gather.7
  208.6 56.4 all-gather.5

commit v2 on v0

v2 whole, which is shorter than its diff:
```python
import functools

import jax
import jax.numpy as jnp
from jax import lax
from jax.experimental import pallas as pl
from jax.experimental.pallas import tpu as pltpu
from jax.sharding import PartitionSpec as P

MESH = pl.DeviceIdType.MESH
HEAD_DIM = 64
BEAMS = 16
STEPS = 2
SEQ = 8
HEAD = 16


def place():
    y = lax.axis_index("src")
    s = lax.axis_index("seq")
    c = lax.axis_index("head")
    zh, k = lax.div(s, 2), lax.rem(s, 2)
    zl, x = lax.div(c, 4), lax.rem(c, 4)
    b, r = lax.rem(zl, 2), lax.div(zl, 2)
    return y, s, c, k, zl, x, b, r, zh * 2 + r


def node_id(m, k, b, x):
    return {"seq": lax.div(m, 2) * 2 + k, "head": (lax.rem(m, 2) * 2 + b) * 4 + x}


def partner_id(s, k):
    return {"seq": s + 1 - 2 * k}


def start_send(sent, src, dst, ss, rs, where):
    copy = pltpu.make_async_remote_copy(
        src_ref=src, dst_ref=dst, send_sem=ss, recv_sem=rs, device_id=where, device_id_type=MESH,
    )
    copy.start()
    sent.append(copy)


def wait_arrival(dst, ss, rs, where):
    pltpu.make_async_remote_copy(
        src_ref=dst, dst_ref=dst, send_sem=ss, recv_sem=rs, device_id=where, device_id_type=MESH,
    ).wait_recv()


OFFSETS = (0, -1, 1, -2, 2, -3, 3, 4)
BY_OFFSET = {off: q for q, off in enumerate(OFFSETS)}


def gather_kernel(
    enc, gain, wk, wv, out,
    ebuf, nbuf, wbuf,
    own_sem, wz_ss, wz_rs, wy_ss, wy_rs, wh_ss, wh_rs, wc_ss, wc_rs, ez_ss, ez_rs, ex_ss, ex_rs, eh_ss, eh_rs,
):
    y, s, c, k, zl, x, b, r, n = place()
    up, down = {"src": lax.rem(y + 1, 4)}, {"src": lax.rem(y + 3, 4)}
    east = {"head": zl * 4 + lax.rem(x + 1, 4)}
    west = {"head": zl * 4 + lax.rem(x + 3, 4)}
    partner = partner_id(s, k)
    right = node_id(lax.rem(n + 1, 8), k, b, x)
    left = node_id(lax.rem(n + 7, 8), k, b, x)
    sibling = zl + 1 - 2 * b
    across = [2 - 2 * r, 3 - 2 * r]
    quarters = [y, lax.rem(y + 3, 4), lax.rem(y + 1, 4), lax.rem(y + 2, 4)]

    def rows_of(m, quarter, core):
        return pl.ds(pl.multiple_of((lax.div(m, 2) * 2 + core) * 512 + quarter * 128, 128), 128)

    def nodes(q):
        return lax.rem(n + 8 + OFFSETS[q], 8)

    def both(q, j, core):
        m = nodes(q)
        return wbuf.at[pl.ds(2 * lax.rem(m, 2), 2), rows_of(m, quarters[j], core), :]

    def one(q, j, mat):
        m = nodes(q)
        return wbuf.at[2 * lax.rem(m, 2) + mat, rows_of(m, quarters[j], k), :]

    def local(src, dst, i):
        copy = pltpu.make_async_copy(src, dst, own_sem.at[i])
        copy.start()
        return copy

    mine = pl.ds(pl.multiple_of(y * 128, 128), 128)
    near = pl.ds(pl.multiple_of(r * 512, 512), 512)
    far = pl.ds(pl.multiple_of(512 - r * 512, 512), 512)
    locals_ = [
        local(wk.at[mine, :], one(0, 0, 0), 0),
        local(wv.at[mine, :], one(0, 0, 1), 1),
        local(enc.at[near, :], ebuf.at[c], 2),
    ]

    barrier = pltpu.get_barrier_semaphore()
    greet = [up, down, east, west, partner, right, left]
    greet += [{"head": zl_to * 4 + x} for zl_to in [sibling] + across]
    for where in greet:
        pl.semaphore_signal(barrier, inc=1, device_id=where, device_id_type=MESH)
    for copy in locals_:
        copy.wait()
    pl.semaphore_wait(barrier, len(greet))

    sent = []
    send = functools.partial(start_send, sent)

    def z_on(q):
        off = OFFSETS[q]
        if off <= 0 and off > -3:
            t = BY_OFFSET[off - 1]
            send(both(q, 0, k), both(q, 0, k), wz_ss.at[t], wz_rs.at[t], right)
        if off >= 0 and off < 3:
            t = BY_OFFSET[off + 1]
            send(both(q, 0, k), both(q, 0, k), wz_ss.at[t], wz_rs.at[t], left)
        if off == -3:
            send(one(q, 0, 0), one(q, 0, 0), wz_ss.at[7], wz_rs.at[7], right)
        if off == 3:
            send(one(q, 0, 1), one(q, 0, 1), wz_ss.at[8], wz_rs.at[8], left)

    def z_in(q):
        off = OFFSETS[q]
        if off == 4:
            wait_arrival(one(q, 0, 0), wz_ss.at[7], wz_rs.at[7], right)
            wait_arrival(one(q, 0, 1), wz_ss.at[8], wz_rs.at[8], left)
        else:
            wait_arrival(both(q, 0, k), wz_ss.at[q], wz_rs.at[q], right)

    def cross(q, j):
        send(both(q, j, k), both(q, j, k), wc_ss.at[q, j], wc_rs.at[q, j], partner)

    def y_out(q):
        send(both(q, 0, k), both(q, 0, k), wy_ss.at[q, 0], wy_rs.at[q, 0], up)
        send(both(q, 0, k), both(q, 0, k), wy_ss.at[q, 1], wy_rs.at[q, 1], down)
        cross(q, 0)

    def y_relay(q):
        wait_arrival(both(q, 1, k), wy_ss.at[q, 0], wy_rs.at[q, 0], up)
        send(one(q, 1, 0), one(q, 1, 0), wh_ss.at[q, 0], wh_rs.at[q, 0], up)
        cross(q, 1)
        wait_arrival(both(q, 2, k), wy_ss.at[q, 1], wy_rs.at[q, 1], down)
        send(one(q, 2, 1), one(q, 2, 1), wh_ss.at[q, 1], wh_rs.at[q, 1], down)
        cross(q, 2)

    def y_last(q):
        wait_arrival(one(q, 3, 0), wh_ss.at[q, 0], wh_rs.at[q, 0], up)
        wait_arrival(one(q, 3, 1), wh_ss.at[q, 1], wh_rs.at[q, 1], down)
        cross(q, 3)

    piece_z = [zl, sibling] + across

    def piece(p, xs):
        return ebuf.at[piece_z[p] * 4 + xs]

    xs = [x, lax.rem(x + 3, 4), lax.rem(x + 1, 4), lax.rem(x + 2, 4)]
    top_half, low_half = pl.ds(0, 256), pl.ds(256, 256)

    def x_out(p):
        send(piece(p, x), piece(p, x), ex_ss.at[p, 0], ex_rs.at[p, 0], east)
        send(piece(p, x), piece(p, x), ex_ss.at[p, 1], ex_rs.at[p, 1], west)

    def x_relay(p):
        wait_arrival(piece(p, xs[1]), ex_ss.at[p, 0], ex_rs.at[p, 0], east)
        part = piece(p, xs[1]).at[top_half, :]
        send(part, part, eh_ss.at[p, 0], eh_rs.at[p, 0], east)
        wait_arrival(piece(p, xs[2]), ex_ss.at[p, 1], ex_rs.at[p, 1], west)
        part = piece(p, xs[2]).at[low_half, :]
        send(part, part, eh_ss.at[p, 1], eh_rs.at[p, 1], west)

    def x_last(p):
        wait_arrival(piece(p, xs[3]).at[top_half, :], eh_ss.at[p, 0], eh_rs.at[p, 0], east)
        wait_arrival(piece(p, xs[3]).at[low_half, :], eh_ss.at[p, 1], eh_rs.at[p, 1], west)

    z_on(0)
    y_out(0)
    send(enc.at[far, :], ebuf.at[c], ez_ss.at[1], ez_rs.at[1 + b], {"head": across[0] * 4 + x})
    send(enc.at[far, :], ebuf.at[c], ez_ss.at[2], ez_rs.at[1 + b], {"head": across[1] * 4 + x})
    send(enc.at[near, :], ebuf.at[c], ez_ss.at[0], ez_rs.at[0], {"head": sibling * 4 + x})
    x_out(0)
    rounds = [[0], [1, 2], [3, 4], [5, 6], [7]]
    for h in range(1, 7):
        if h < 5:
            for q in rounds[h]:
                z_in(q)
                z_on(q)
                y_out(q)
        if h < 4:
            wait_arrival(piece(h, x), ez_ss.at[h - 1], ez_rs.at[h - 1], east)
            x_out(h)
        if h - 1 < 5:
            for q in rounds[h - 1]:
                y_relay(q)
        if h - 1 < 4:
            x_relay(h - 1)
        if h >= 2:
            for q in rounds[h - 2]:
                y_last(q)
            if h - 2 < 4:
                x_last(h - 2)
    for q in range(8):
        for j in range(4):
            wait_arrival(both(q, j, 1 - k), wc_ss.at[q, j], wc_rs.at[q, j], partner)

    @pl.loop(0, 8)
    def _(i):
        at = pl.ds(pl.multiple_of(i * 64, 64), 64)
        acc = jnp.zeros((64, 128), jnp.float32)
        for f in range(HEAD):
            part = ebuf[f, at, :].astype(jnp.float32)
            part = part * part
            acc += part[:, :128] + part[:, 128:]
        scale = lax.rsqrt(jnp.sum(acc, axis=-1, keepdims=True) * (1.0 / 4096.0) + 1e-06)
        for f in range(HEAD):
            part = ebuf[f, at, :].astype(jnp.float32) * scale * gain[f:f + 1, :]
            nbuf[at, 256 * f:256 * f + 256] = part.astype(jnp.bfloat16)

    @pl.loop(0, 4)
    def _(i):
        out[i] = jnp.dot(nbuf[...], wbuf[i], preferred_element_type=jnp.float32).astype(jnp.bfloat16)

    for copy in sent:
        copy.wait_send()


def gather(enc, gain, wk, wv):
    vmem = pl.BlockSpec(memory_space=pltpu.VMEM)
    bf16 = jnp.bfloat16
    dma = pltpu.SemaphoreType.DMA
    return pl.pallas_call(
        gather_kernel,
        out_shape=jax.ShapeDtypeStruct((4, 512, 256), bf16),
        in_specs=[vmem] * 4,
        out_specs=vmem,
        scratch_shapes=[
            pltpu.VMEM((HEAD, 512, 256), bf16),
            pltpu.VMEM((512, 4096), bf16),
            pltpu.VMEM((4, 4096, 256), bf16),
            dma((3,)),
            dma((9,)), dma((9,)),
            dma((8, 2)), dma((8, 2)),
            dma((8, 2)), dma((8, 2)),
            dma((8, 4)), dma((8, 4)),
            dma((3,)), dma((3,)),
            dma((4, 2)), dma((4, 2)),
            dma((4, 2)), dma((4, 2)),
        ],
        compiler_params=pltpu.CompilerParams(collective_id=2, has_side_effects=True),
        name="gather",
    )(enc, gain, wk, wv)


def decode_kernel(
    kv, wq, wo, gain, first, parents, tokens,
    out_state, out_att,
    state, nrm, q_own, q_all, u_own, u_all, c_own, c_all, t_own, t_all, m_own, m_all, v_own, v_all,
    p_own, p_all, f_own, f_all, g_all,
    q_ss, q_rs, u_ss, u_rs, c_ss, c_rs, t_ss, t_rs, m_ss, m_rs, v_ss, v_rs, p_ss, p_rs, f_ss, f_rs, g_ss, g_rs,
):
    y, s, c, k, zl, x, b, r, n = place()
    seq_peers = [lax.rem(s + i, SEQ) for i in range(1, SEQ)]
    head_peers = [lax.rem(c + i, HEAD) for i in range(1, HEAD)]
    ring_peers = [lax.rem(n + i, 8) for i in range(1, 8)]
    partner = partner_id(s, k)
    other = 1 - k

    def ring(m):
        return node_id(m, k, b, x)

    barrier = pltpu.get_barrier_semaphore()
    greet = [{"seq": p} for p in seq_peers] + [{"head": p} for p in head_peers]
    greet += [ring(m) for m in ring_peers]
    for where in greet:
        pl.semaphore_signal(barrier, inc=1, device_id=where, device_id_type=MESH)
    pl.semaphore_wait(barrier, len(greet))

    sent = []
    send = functools.partial(start_send, sent)

    col_head = lax.broadcasted_iota(jnp.int32, (BEAMS, 256), 1) // HEAD_DIM
    lane = lax.broadcasted_iota(jnp.int32, (8, 128), 1)

    def spread_rows(share):
        halves = []
        for half in range(2):
            scale = jnp.zeros((8, 256), jnp.float32)
            for h in range(4):
                at = 8 * half + h
                scale = jnp.where(
                    col_head[:8] == h, jnp.broadcast_to(share[:, at:at + 1], (8, 256)), scale
                )
            halves.append(scale)
        return jnp.concatenate(halves, axis=0)

    def merge(stats, parts):
        peak = functools.reduce(jnp.maximum, stats)
        factors = [jnp.exp(one - peak) for one in stats]
        sums = functools.reduce(
            lambda a, b: a + b, [f * pltpu.roll(one, 124, 1) for f, one in zip(factors, stats)]
        )
        joined = functools.reduce(
            lambda a, b: a + b, [part * spread_rows(f) for f, part in zip(factors, parts)]
        )
        return peak, sums, joined

    is_top = lax.rem(lane, 8) < 4

    for t in range(STEPS):
        for i in range(BEAMS):
            source = first[parents[t, i]] if t == 0 else state[t - 1, parents[t, i]]
            row = source + tokens[t, i]
            square = jnp.sum(jnp.sum(row * row, axis=0), axis=(0, 1), keepdims=True) * (1.0 / 4096.0)
            state[t, i] = row
            nrm[i] = row * lax.rsqrt(square + 1e-06)[None] * gain[...]
        part = jnp.zeros((BEAMS, 256), jnp.float32)
        for j in range(4):
            part += jnp.dot(
                nrm[:, s, j, :].astype(jnp.bfloat16), wq[pl.ds(128 * j, 128), :],
                preferred_element_type=jnp.float32,
            )
        q_own[t] = part
        q_all[t, n] = part
        for i, m in enumerate(ring_peers):
            send(q_own.at[t], q_all.at[t, n], q_ss.at[t, i], q_rs.at[t, n], ring(m))
        for i, m in enumerate(ring_peers):
            wait_arrival(q_all.at[t, m], q_ss.at[t, i], q_rs.at[t, m], ring(m))
        for g in range(2):
            u_all[t, k, g] = (q_all[t, g] + q_all[t, g + 2]) + (q_all[t, g + 4] + q_all[t, g + 6])
            u_own[t, g] = u_all[t, k, g]
        send(u_own.at[t], u_all.at[t, k], u_ss.at[t], u_rs.at[t], partner)
        wait_arrival(u_all.at[t, other], u_ss.at[t], u_rs.at[t], partner)
        for g in range(2):
            query = (u_all[t, 0, g] + u_all[t, 1, g]).astype(jnp.bfloat16).astype(jnp.float32)
            spread = jnp.concatenate(
                [jnp.where(col_head == h, query, 0.0) for h in range(4)], axis=0
            ).astype(jnp.bfloat16)
            scores = lax.dot_general(
                spread, kv[2 * g], (((1,), (1,)), ((), ())), preferred_element_type=jnp.float32
            ) * 0.125
            top = jnp.max(scores, axis=-1, keepdims=True)
            expo = jnp.exp(scores - top)
            total = jnp.sum(expo, axis=-1, keepdims=True)
            mixed = jnp.dot(
                expo.astype(jnp.bfloat16), kv[2 * g + 1], preferred_element_type=jnp.float32
            )
            ctx = jnp.zeros((BEAMS, 256), jnp.float32)
            stats = jnp.zeros((8, 128), jnp.float32)
            for h in range(4):
                ctx += jnp.where(col_head == h, mixed[16 * h:16 * h + 16], 0.0)
                for half in range(2):
                    at = 16 * h + 8 * half
                    stats = jnp.where(lane == 8 * half + h, top[at:at + 8], stats)
                    stats = jnp.where(lane == 8 * half + 4 + h, total[at:at + 8], stats)
            c_own[t, g] = ctx.astype(jnp.bfloat16)
            t_own[t, g] = stats
        c_all[t, n] = c_own[t, r]
        t_all[t, n] = t_own[t, r]
        for i, m in enumerate(ring_peers):
            g = lax.rem(m, 2)
            send(t_own.at[t, g], t_all.at[t, n], t_ss.at[t, i], t_rs.at[t, n], ring(m))
            send(c_own.at[t, g], c_all.at[t, n], c_ss.at[t, i], c_rs.at[t, n], ring(m))
        for i, m in enumerate(ring_peers):
            wait_arrival(t_all.at[t, m], t_ss.at[t, i], t_rs.at[t, m], ring(m))
            wait_arrival(c_all.at[t, m], c_ss.at[t, i], c_rs.at[t, m], ring(m))
        peak, sums, joined = merge(
            [t_all[t, i] for i in range(8)], [c_all[t, i].astype(jnp.float32) for i in range(8)]
        )
        stats = jnp.where(is_top, peak, pltpu.roll(sums, 4, 1))
        v_own[t] = joined
        m_own[t] = stats
        v_all[t, k] = joined
        m_all[t, k] = stats
        send(m_own.at[t], m_all.at[t, k], m_ss.at[t], m_rs.at[t], partner)
        send(v_own.at[t], v_all.at[t, k], v_ss.at[t], v_rs.at[t], partner)
        wait_arrival(m_all.at[t, other], m_ss.at[t], m_rs.at[t], partner)
        wait_arrival(v_all.at[t, other], v_ss.at[t], v_rs.at[t], partner)
        peak, sums, joined = merge([m_all[t, 0], m_all[t, 1]], [v_all[t, 0], v_all[t, 1]])
        context = (joined / spread_rows(sums)).astype(jnp.bfloat16)
        partial = jnp.dot(context, wo[...], preferred_element_type=jnp.float32)
        for j in range(4):
            p_own[t, :, j, :] = partial[:, 128 * j:128 * j + 128]
        p_all[t, c] = p_own[t, c]
        for i, p in enumerate(head_peers):
            send(p_own.at[t, p], p_all.at[t, c], p_ss.at[t, i], p_rs.at[t, c], {"head": p})
        for i, p in enumerate(head_peers):
            wait_arrival(p_all.at[t, p], p_ss.at[t, i], p_rs.at[t, p], {"head": p})
        row = p_all[t, 0]
        for i in range(1, HEAD):
            row += p_all[t, i]
        f_own[t] = row
        f_all[t, s] = row
        for i, p in enumerate(seq_peers):
            send(f_own.at[t], f_all.at[t, s], f_ss.at[t, i], f_rs.at[t, s], {"seq": p})
        for i, p in enumerate(seq_peers):
            wait_arrival(f_all.at[t, p], f_ss.at[t, i], f_rs.at[t, p], {"seq": p})
        for i, p in enumerate(head_peers):
            send(f_all.at[t], g_all.at[t, c], g_ss.at[t, i], g_rs.at[t, c], {"head": p})
        g_all[t, c] = f_all[t]
        for i, p in enumerate(head_peers):
            wait_arrival(g_all.at[t, p], g_ss.at[t, i], g_rs.at[t, p], {"head": p})
        for i in range(BEAMS):
            state[t, i] = state[t, i] + g_all[t, i]
    for i in range(BEAMS):
        out_state[i] = state[STEPS - 1, i]
        out_att[i] = g_all[0, i] + g_all[1, i]
    for copy in sent:
        copy.wait_send()


def decode(kv, wq, wo, gain, first, parents, tokens):
    vmem = pl.BlockSpec(memory_space=pltpu.VMEM)
    f32, bf16 = jnp.float32, jnp.bfloat16
    dma = pltpu.SemaphoreType.DMA
    rows = jax.ShapeDtypeStruct((BEAMS, 8, 4, 128), f32)
    return pl.pallas_call(
        decode_kernel,
        out_shape=(rows, rows),
        in_specs=[vmem] * 5 + [pl.BlockSpec(memory_space=pltpu.SMEM), vmem],
        out_specs=(vmem, vmem),
        scratch_shapes=[
            pltpu.VMEM((STEPS, BEAMS, 8, 4, 128), f32),
            pltpu.VMEM((BEAMS, 8, 4, 128), f32),
            pltpu.VMEM((STEPS, BEAMS, 256), f32),
            pltpu.VMEM((STEPS, 8, BEAMS, 256), f32),
            pltpu.VMEM((STEPS, 2, BEAMS, 256), f32),
            pltpu.VMEM((STEPS, 2, 2, BEAMS, 256), f32),
            pltpu.VMEM((STEPS, 2, BEAMS, 256), bf16),
            pltpu.VMEM((STEPS, 8, BEAMS, 256), bf16),
            pltpu.VMEM((STEPS, 2, 8, 128), f32),
            pltpu.VMEM((STEPS, 8, 8, 128), f32),
            pltpu.VMEM((STEPS, 8, 128), f32),
            pltpu.VMEM((STEPS, 2, 8, 128), f32),
            pltpu.VMEM((STEPS, BEAMS, 256), f32),
            pltpu.VMEM((STEPS, 2, BEAMS, 256), f32),
            pltpu.VMEM((STEPS, BEAMS, 4, 128), f32),
            pltpu.VMEM((STEPS, HEAD, 4, 128), f32),
            pltpu.VMEM((STEPS, 4, 128), f32),
            pltpu.VMEM((STEPS, SEQ, 4, 128), f32),
            pltpu.VMEM((STEPS, BEAMS, 8, 4, 128), f32),
            dma((STEPS, 8)), dma((STEPS, 8)),
            dma((STEPS,)), dma((STEPS,)),
            dma((STEPS, 8)), dma((STEPS, 8)),
            dma((STEPS, 8)), dma((STEPS, 8)),
            dma((STEPS,)), dma((STEPS,)),
            dma((STEPS,)), dma((STEPS,)),
            dma((STEPS, HEAD)), dma((STEPS, HEAD)),
            dma((STEPS, SEQ)), dma((STEPS, SEQ)),
            dma((STEPS, HEAD)), dma((STEPS, HEAD)),
        ],
        compiler_params=pltpu.CompilerParams(collective_id=1, has_side_effects=True),
        name="decode",
    )(kv, wq, wo, gain, first, parents, tokens)


def on_device(
    enc_out, enc_gain, key_weight, value_weight, query_weight, out_weight,
    dec_gain, beam_state, parents, token_embed,
):
    kv = gather(enc_out, enc_gain.reshape(HEAD, 256), key_weight, value_weight)
    state, attended = decode(
        kv, query_weight, out_weight,
        dec_gain.reshape(8, 4, 128),
        beam_state.reshape(BEAMS, 8, 4, 128),
        parents,
        token_embed.astype(jnp.float32).reshape(STEPS, BEAMS, 8, 4, 128),
    )
    return state.reshape(BEAMS, 4096), attended.reshape(BEAMS, 4096)


def solution(mesh):
    placed = (
        P(("src", "seq"), "head"),
        P(),
        P("seq", "head"),
        P("seq", "head"),
        P("seq", "head"),
        P("head", "seq"),
        P(),
        P("src", None),
        P("src", None),
        P("src", None, None),
    )
    return jax.shard_map(
        on_device,
        mesh=mesh,
        in_specs=placed,
        out_specs=(P("src", None), P("src", None)),
        check_vma=False,
    )
```

time: 603 us -> 189 us (0.31); the launches traced: 593 us -> 187 us
  blocking collectives: 378 us -> 0 us
  Pallas kernels: 0 us -> 180 us
  waiting for transfers between devices: 174 us -> 0 us
  matrix products: 15.9 us -> 0 us
  between operations: 13.9 us -> 0.66 us
  other arithmetic: 8.64 us -> 0 us
    psum x6 -> x0, blocking collectives: 301 us -> none  [the longest x2 142 us: on_device(): lax.psum(partial_out.astype(jnp.bfloat16), 'head').astype(jnp.float32)]
    pallas_call x0 -> x2, Pallas kernels: none -> 180 us  [the longest x1 97.4 us: decode(): pl.pallas_call(decode_kernel, out_shape=(rows, rows), in_specs=[vmem] * 5...]
    all_gather x3 -> x0, waiting for transfers between devices: 172 us -> none  [the longest x1 85 us: on_device(): full_rows = lax.all_gather(enc_out, 'head', axis=1, tiled=True)]
    pmax x2 -> x0, blocking collectives: 39.5 us -> none  [on_device(): peak_all = lax.pmax(top, 'seq')]
    all_gather x2 -> x0, blocking collectives: 36.8 us -> none  [on_device(): lax.all_gather(columns.astype(jnp.bfloat16), 'seq', axis=1, tiled=True)]
    dot_general x10 -> x0, matrix products: 15.9 us -> none  [the longest x1 6.63 us: on_device(): jnp.dot(memory, key_full, preferred_element_type=jnp.float32)]
    reduce_sum x5 -> x0, other arithmetic: 6.8 us -> none  [the longest x3 6.43 us: rms_norm(): mean_square = jnp.mean(values * values, axis=-1, keepdims=True)]
    reshape x4 -> x5, local copies, waits for them, and re-layouts: 0.36 us -> 7.01 us  [the longest x2 2.61 us: on_device(): return (state.reshape(BEAMS, 4096), attended.reshape(BEAMS, 4096))]
  transfers between devices with their start and end apart: 3 -> 0, of which waited for: 3 -> 0; matrix products, arithmetic and copies ran while one was open for 3% -> 0% of each run, Pallas kernels for 0% -> 0%
where the time goes in v2:
time: 189 us; the launch traced here: 187 us
  Pallas kernels  180 us (95%)
  local copies, waits for them, and re-layouts  7.02 us (4%)
    pallas_call x1, Pallas kernels, decode(): pl.pallas_call(decode_kernel, out_shape=(rows, rows), in_specs=[vmem] * 5...  97.4 us
    pallas_call x1, Pallas kernels, gather(): pl.pallas_call(gather_kernel, out_shape=jax.ShapeDtypeStruct((4, 512, 256...  82.3 us

profile of v2, /device:TPU:6, one launch (start us, length us, event | category | flops | bytes accessed | tf_op | source)
XLA Modules:
  0.0 187.3 jit_solution(6490367461922280742)
XLA Ops:
  0.6 1.3 reshape.24.gain
  2.0 0.0 copy-start
  2.0 1.9 %reshape.26.first = f32[16,8,4,128]{3,2,1,0:T(4,128)} reshape(f32[16,4096]{1,0:T(8,128)} %param.17) | data formatting | bytes 524288 | tf_op jit(solution)/shard_map/reshape | solution.py:464
  3.8 0.0 copy-done
  3.8 1.2 reshape.32.tokens
  5.0 82.3 %gather.1.kv = bf16[4,512,256]{2,1,0:T(8,128)(2,1)} custom-call(bf16[1024,256]{1,0:T(8,128)(2,1)} %enc.1, f32[16,256]{1,0:T(8,128)} %reshape.24.gain, bf16[512,256]{1,0:T(8,128)(2,1)} %wk.1, bf16[512,256]{1,0:T(8,128)(2,1)} %wv.1), custom_call_target="tpu_custom_call" | custom-call | tf_op jit(solution)/shard_map/gather/pallas_call | solution.py:231
  87.3 97.4 %decode.1 = (f32[16,8,4,128]{3,2,1,0:T(4,128)}, f32[16,8,4,128]{3,2,1,0:T(4,128)}) custom-call(bf16[4,512,256]{2,1,0:T(8,128)(2,1)} %gather.1.kv, bf16[512,256]{1,0:T(8,128)(2,1)} %wq.1, bf16[256,512]{1,0:T(8,128)(2,1)} %wo.1, f32[8,4,128]{2,1,0:T(4,128)} %bitcast.1, f32[16,8,4,128]{3,2,1,0:T(4,128)} %reshape.26.first, s32[2,16]{1,0:T(2,128)} %parents.1, ...), custom_call_target="tpu_custom_call" | custom-call | tf_op jit(solution)/shard_map/decode/pallas_call | solution.py:416
  184.7 0.0 copy-start.1
  184.7 1.8 reshape.29
  186.5 0.0 copy-done.1
  186.5 0.8 reshape.30
Async XLA Ops:
  2.0 1.9 %copy-start = (bf16[2,16,4096]{2,1,0:T(8,128)(2,1)S(1)}, bf16[2,16,4096]{2,1,0:T(8,128)(2,1)}, u32[]{:S(2)}) copy-start(bf16[2,16,4096]{2,1,0:T(8,128)(2,1)} %param.19) | copy-start | bytes 786436
  184.7 1.8 copy-start.1

commit v3 on v2

v3 whole, which is shorter than its diff:
```python
import functools

import jax
import jax.numpy as jnp
from jax import lax
from jax.experimental import pallas as pl
from jax.experimental.pallas import tpu as pltpu
from jax.sharding import PartitionSpec as P

MESH = pl.DeviceIdType.MESH
HEAD_DIM = 64
BEAMS = 16
STEPS = 2
SEQ = 8
HEAD = 16


def place():
    y = lax.axis_index("src")
    s = lax.axis_index("seq")
    c = lax.axis_index("head")
    zh, k = lax.div(s, 2), lax.rem(s, 2)
    zl, x = lax.div(c, 4), lax.rem(c, 4)
    b, r = lax.rem(zl, 2), lax.div(zl, 2)
    return y, s, c, k, zl, x, b, r, zh * 2 + r


def node_id(m, k, b, x):
    return {"seq": lax.div(m, 2) * 2 + k, "head": (lax.rem(m, 2) * 2 + b) * 4 + x}


def partner_id(s, k):
    return {"seq": s + 1 - 2 * k}


def start_send(sent, src, dst, ss, rs, where):
    copy = pltpu.make_async_remote_copy(
        src_ref=src, dst_ref=dst, send_sem=ss, recv_sem=rs, device_id=where, device_id_type=MESH,
    )
    copy.start()
    sent.append(copy)


def wait_arrival(dst, ss, rs, where):
    pltpu.make_async_remote_copy(
        src_ref=dst, dst_ref=dst, send_sem=ss, recv_sem=rs, device_id=where, device_id_type=MESH,
    ).wait_recv()


OFFSETS = (0, -1, 1, -2, 2, -3, 3, 4)
BY_OFFSET = {off: q for q, off in enumerate(OFFSETS)}


def kernel(
    enc, enc_gain, wk, wv, wq, wo, gain, first, parents, tokens,
    out_state, out_att,
    ebuf, nbuf, wbuf, kv,
    pre, part, picked, local_rows, full,
    q_own, q_all, u_own, u_all, z_own, z_all, zz_own, zz_all, c_own, c_all, t_own, t_all, m_own, m_all, v_own, v_all,
    p_own, p_all, f_own, f_all, l_all, g_all,
    own_sem, wz_ss, wz_rs, wy_ss, wy_rs, wh_ss, wh_rs, wc_ss, wc_rs, ez_ss, ez_rs, ex_ss, ex_rs, eh_ss, eh_rs,
    q_ss, q_rs, u_ss, u_rs, z_ss, z_rs, zz_ss, zz_rs, c_ss, c_rs, t_ss, t_rs, m_ss, m_rs, v_ss, v_rs,
    p_ss, p_rs, f_ss, f_rs, l_ss, l_rs, g_ss, g_rs,
):
    y, s, c, k, zl, x, b, r, n = place()
    up, down = {"src": lax.rem(y + 1, 4)}, {"src": lax.rem(y + 3, 4)}
    east = {"head": zl * 4 + lax.rem(x + 1, 4)}
    west = {"head": zl * 4 + lax.rem(x + 3, 4)}
    partner = partner_id(s, k)
    right = node_id(lax.rem(n + 1, 8), k, b, x)
    left = node_id(lax.rem(n + 7, 8), k, b, x)
    sibling = zl + 1 - 2 * b
    opposite = lax.rem(zl + 2, 4)
    quarters = [y, lax.rem(y + 3, 4), lax.rem(y + 1, 4), lax.rem(y + 2, 4)]

    def rows_of(m, quarter, core):
        return pl.ds(pl.multiple_of((lax.div(m, 2) * 2 + core) * 512 + quarter * 128, 128), 128)

    def nodes(q):
        return lax.rem(n + 8 + OFFSETS[q], 8)

    def both(q, j, core):
        m = nodes(q)
        return wbuf.at[pl.ds(2 * lax.rem(m, 2), 2), rows_of(m, quarters[j], core), :]

    def one(q, j, mat):
        m = nodes(q)
        return wbuf.at[2 * lax.rem(m, 2) + mat, rows_of(m, quarters[j], k), :]

    def local(src, dst, i):
        copy = pltpu.make_async_copy(src, dst, own_sem.at[i])
        copy.start()
        return copy

    mine = pl.ds(pl.multiple_of(y * 128, 128), 128)
    near = pl.ds(pl.multiple_of(r * 512, 512), 512)
    far = pl.ds(pl.multiple_of(512 - r * 512, 512), 512)
    locals_ = [
        local(wk.at[mine, :], one(0, 0, 0), 0),
        local(wv.at[mine, :], one(0, 0, 1), 1),
        local(enc.at[near, :], ebuf.at[c], 2),
    ]

    seq_peers = [lax.rem(s + i, SEQ) for i in range(1, SEQ)]
    head_peers = [lax.rem(c + i, HEAD) for i in range(1, HEAD)]
    ring_peers = [lax.rem(n + i, 8) for i in range(1, 8)]
    other = 1 - k
    feats = pl.ds(pl.multiple_of(s * 512, 512), 512)

    def ring(m):
        return node_id(m, k, b, x)

    barrier = pltpu.get_barrier_semaphore()
    greet = [up, down]
    greet += [{"seq": p} for p in seq_peers] + [{"head": p} for p in head_peers]
    greet += [ring(m) for m in ring_peers]
    for where in greet:
        pl.semaphore_signal(barrier, inc=1, device_id=where, device_id_type=MESH)
    for copy in locals_:
        copy.wait()
    pl.semaphore_wait(barrier, len(greet))

    sent = []
    send = functools.partial(start_send, sent)

    def z_on(q):
        off = OFFSETS[q]
        if off <= 0 and off > -3:
            t = BY_OFFSET[off - 1]
            send(both(q, 0, k), both(q, 0, k), wz_ss.at[t], wz_rs.at[t], right)
        if off >= 0 and off < 3:
            t = BY_OFFSET[off + 1]
            send(both(q, 0, k), both(q, 0, k), wz_ss.at[t], wz_rs.at[t], left)
        if off == -3:
            send(one(q, 0, 0), one(q, 0, 0), wz_ss.at[7], wz_rs.at[7], right)
        if off == 3:
            send(one(q, 0, 1), one(q, 0, 1), wz_ss.at[8], wz_rs.at[8], left)

    def z_in(q):
        off = OFFSETS[q]
        if off == 4:
            wait_arrival(one(q, 0, 0), wz_ss.at[7], wz_rs.at[7], right)
            wait_arrival(one(q, 0, 1), wz_ss.at[8], wz_rs.at[8], left)
        else:
            wait_arrival(both(q, 0, k), wz_ss.at[q], wz_rs.at[q], right)

    def cross(q, j):
        send(both(q, j, k), both(q, j, k), wc_ss.at[q, j], wc_rs.at[q, j], partner)

    def y_out(q):
        send(both(q, 0, k), both(q, 0, k), wy_ss.at[q, 0], wy_rs.at[q, 0], up)
        send(both(q, 0, k), both(q, 0, k), wy_ss.at[q, 1], wy_rs.at[q, 1], down)
        cross(q, 0)

    def y_relay(q):
        wait_arrival(both(q, 1, k), wy_ss.at[q, 0], wy_rs.at[q, 0], up)
        send(one(q, 1, 0), one(q, 1, 0), wh_ss.at[q, 0], wh_rs.at[q, 0], up)
        cross(q, 1)
        wait_arrival(both(q, 2, k), wy_ss.at[q, 1], wy_rs.at[q, 1], down)
        send(one(q, 2, 1), one(q, 2, 1), wh_ss.at[q, 1], wh_rs.at[q, 1], down)
        cross(q, 2)

    def y_last(q):
        wait_arrival(one(q, 3, 0), wh_ss.at[q, 0], wh_rs.at[q, 0], up)
        wait_arrival(one(q, 3, 1), wh_ss.at[q, 1], wh_rs.at[q, 1], down)
        cross(q, 3)

    piece_z = [zl, sibling, opposite, lax.rem(sibling + 2, 4)]

    def piece(p, xs):
        return ebuf.at[piece_z[p] * 4 + xs]

    xs = [x, lax.rem(x + 3, 4), lax.rem(x + 1, 4), lax.rem(x + 2, 4)]
    top_half, low_half = pl.ds(0, 256), pl.ds(256, 256)

    def x_out(p):
        send(piece(p, x), piece(p, x), ex_ss.at[p, 0], ex_rs.at[p, 0], east)
        send(piece(p, x), piece(p, x), ex_ss.at[p, 1], ex_rs.at[p, 1], west)

    def x_relay(p):
        wait_arrival(piece(p, xs[1]), ex_ss.at[p, 0], ex_rs.at[p, 0], east)
        part = piece(p, xs[1]).at[top_half, :]
        send(part, part, eh_ss.at[p, 0], eh_rs.at[p, 0], east)
        wait_arrival(piece(p, xs[2]), ex_ss.at[p, 1], ex_rs.at[p, 1], west)
        part = piece(p, xs[2]).at[low_half, :]
        send(part, part, eh_ss.at[p, 1], eh_rs.at[p, 1], west)

    def x_last(p):
        wait_arrival(piece(p, xs[3]).at[top_half, :], eh_ss.at[p, 0], eh_rs.at[p, 0], east)
        wait_arrival(piece(p, xs[3]).at[low_half, :], eh_ss.at[p, 1], eh_rs.at[p, 1], west)

    col_head = lax.broadcasted_iota(jnp.int32, (BEAMS, 256), 1) // HEAD_DIM
    lane = lax.broadcasted_iota(jnp.int32, (8, 128), 1)
    is_top = lax.rem(lane, 8) < 4

    def spread_rows(share):
        halves = []
        for half in range(2):
            scale = jnp.zeros((8, 256), jnp.float32)
            for h in range(4):
                at = 8 * half + h
                scale = jnp.where(
                    col_head[:8] == h, jnp.broadcast_to(share[:, at:at + 1], (8, 256)), scale
                )
            halves.append(scale)
        return jnp.concatenate(halves, axis=0)

    def merge(stats, parts):
        peak = functools.reduce(jnp.maximum, stats)
        factors = [jnp.exp(one - peak) for one in stats]
        sums = functools.reduce(
            lambda a, b: a + b, [f * pltpu.roll(one, 124, 1) for f, one in zip(factors, stats)]
        )
        joined = functools.reduce(
            lambda a, b: a + b, [one * spread_rows(f) for f, one in zip(factors, parts)]
        )
        return peak, sums, joined

    def query_out(t):
        for i, m in enumerate(ring_peers):
            if t == 1:
                send(z_own, z_all.at[n], z_ss.at[i], z_rs.at[n], ring(m))
            send(q_own.at[t], q_all.at[t, n], q_ss.at[t, i], q_rs.at[t, n], ring(m))

    def query_swap(t):
        for i, m in enumerate(ring_peers):
            if t == 1:
                wait_arrival(z_all.at[m], z_ss.at[i], z_rs.at[m], ring(m))
            wait_arrival(q_all.at[t, m], q_ss.at[t, i], q_rs.at[t, m], ring(m))
        if t == 1:
            squares = (z_all[0] + z_all[2]) + (z_all[4] + z_all[6])
            zz_own[...] = squares
            zz_all[k] = squares
            send(zz_own, zz_all.at[k], zz_ss.at[0], zz_rs.at[0], partner)
        for g in range(2):
            both_g = (q_all[t, g] + q_all[t, g + 2]) + (q_all[t, g + 4] + q_all[t, g + 6])
            u_all[t, k, g] = both_g
            u_own[t, g] = both_g
        send(u_own.at[t], u_all.at[t, k], u_ss.at[t], u_rs.at[t], partner)

    def query_in(t):
        if t == 1:
            wait_arrival(zz_all.at[other], zz_ss.at[0], zz_rs.at[0], partner)
        wait_arrival(u_all.at[t, other], u_ss.at[t], u_rs.at[t], partner)

    def attend(t, g, scale):
        query = u_all[t, 0, g] + u_all[t, 1, g]
        if scale is not None:
            query = query * scale
        query = query.astype(jnp.bfloat16).astype(jnp.float32)
        spread = jnp.concatenate(
            [jnp.where(col_head == h, query, 0.0) for h in range(4)], axis=0
        ).astype(jnp.bfloat16)
        scores = lax.dot_general(
            spread, kv[2 * g], (((1,), (1,)), ((), ())), preferred_element_type=jnp.float32
        ) * 0.125
        top = jnp.max(scores, axis=-1, keepdims=True)
        expo = jnp.exp(scores - top)
        total = jnp.sum(expo, axis=-1, keepdims=True)
        mixed = jnp.dot(expo.astype(jnp.bfloat16), kv[2 * g + 1], preferred_element_type=jnp.float32)
        ctx = jnp.zeros((BEAMS, 256), jnp.float32)
        stats = jnp.zeros((8, 128), jnp.float32)
        for h in range(4):
            ctx += jnp.where(col_head == h, mixed[16 * h:16 * h + 16], 0.0)
            for half in range(2):
                at = 16 * h + 8 * half
                stats = jnp.where(lane == 8 * half + h, top[at:at + 8], stats)
                stats = jnp.where(lane == 8 * half + 4 + h, total[at:at + 8], stats)
        return ctx.astype(jnp.bfloat16), stats

    z_on(0)
    send(enc.at[near, :], ebuf.at[c], ez_ss.at[0], ez_rs.at[0], {"head": sibling * 4 + x})
    send(enc.at[far, :], ebuf.at[c], ez_ss.at[1], ez_rs.at[1], {"head": opposite * 4 + x})
    y_out(0)
    x_out(0)

    for i in range(BEAMS):
        picked[pl.ds(i, 1), :] = first[pl.ds(parents[0, i], 1), :]
    start = picked[...] + tokens[0].astype(jnp.float32)
    pre[...] = start
    mean = jnp.sum(start * start, axis=-1, keepdims=True) * (1.0 / 4096.0)
    picked[...] = start * lax.rsqrt(mean + 1e-06) * gain[...]
    q_own[0] = jnp.dot(picked[:, feats].astype(jnp.bfloat16), wq[...], preferred_element_type=jnp.float32)
    q_all[0, n] = q_own[0]
    query_out(0)

    def weights_round(qs):
        for q in qs:
            z_in(q)
            z_on(q)
            y_out(q)

    weights_round([1, 2])
    y_relay(0)
    x_relay(0)
    wait_arrival(piece(1, x), ez_ss.at[0], ez_rs.at[0], east)
    x_out(1)
    wait_arrival(piece(2, x), ez_ss.at[1], ez_rs.at[1], east)
    send(piece(2, x), piece(2, x), ez_ss.at[2], ez_rs.at[2], {"head": sibling * 4 + x})
    x_out(2)
    weights_round([3, 4])
    y_relay(1)
    y_relay(2)
    y_last(0)
    x_relay(1)
    x_last(0)
    weights_round([5, 6])
    wait_arrival(piece(3, x), ez_ss.at[2], ez_rs.at[2], east)
    x_out(3)
    y_relay(3)
    y_relay(4)
    x_relay(2)
    y_last(1)
    y_last(2)
    x_last(1)
    weights_round([7])
    query_swap(0)
    y_relay(5)
    y_relay(6)
    x_relay(3)
    y_last(3)
    y_last(4)
    x_last(2)
    y_relay(7)
    y_last(5)
    y_last(6)
    x_last(3)
    y_last(7)

    @pl.loop(0, 8)
    def _(i):
        at = pl.ds(pl.multiple_of(i * 64, 64), 64)
        acc = jnp.zeros((64, 128), jnp.float32)
        for f in range(HEAD):
            block = ebuf[f, at, :].astype(jnp.float32)
            block = block * block
            acc += block[:, :128] + block[:, 128:]
        scale = lax.rsqrt(jnp.sum(acc, axis=-1, keepdims=True) * (1.0 / 4096.0) + 1e-06)
        for f in range(HEAD):
            cols = slice(256 * f, 256 * f + 256)
            block = ebuf[f, at, :].astype(jnp.float32) * scale * enc_gain[:, cols]
            nbuf[at, cols] = block.astype(jnp.bfloat16)

    for q in range(8):
        for j in range(4):
            wait_arrival(both(q, j, other), wc_ss.at[q, j], wc_rs.at[q, j], partner)

    @pl.loop(0, 4)
    def _(i):
        kv[i] = jnp.dot(nbuf[...], wbuf[i], preferred_element_type=jnp.float32).astype(jnp.bfloat16)

    for t in range(STEPS):
        scale = None
        if t == 1:
            for j in range(4):
                part[:, 128 * j:128 * j + 128] = l_all[:, j, :]
            part[...] = part[...] + pre[:, feats]
            for i in range(BEAMS):
                local_rows[pl.ds(i, 1), :] = part[pl.ds(parents[1, i], 1), :]
            rows = local_rows[...] + tokens[1, :, feats].astype(jnp.float32)
            squares = jnp.sum(rows * rows, axis=-1, keepdims=True)
            z_own[...] = jnp.where(lane < 64, squares[:8], squares[8:])
            z_all[n] = z_own[...]
            scaled = rows * gain[:, feats]
            high = scaled.astype(jnp.bfloat16)
            low = (scaled - high.astype(jnp.float32)).astype(jnp.bfloat16)
            q_own[1] = jnp.dot(high, wq[...], preferred_element_type=jnp.float32) + jnp.dot(
                low, wq[...], preferred_element_type=jnp.float32
            )
            q_all[1, n] = q_own[1]
            query_out(1)
            query_swap(1)
            for i, p in enumerate(seq_peers):
                wait_arrival(f_all.at[0, p], f_ss.at[0, i], f_rs.at[0, p], {"seq": p})
            for i, p in enumerate(head_peers):
                send(f_all.at[0], g_all.at[0, c], g_ss.at[0, i], g_rs.at[0, c], {"head": p})
            g_all[0, c] = f_all[0]
        query_in(t)
        if t == 1:
            table = lax.rsqrt((zz_all[0] + zz_all[1]) * (1.0 / 4096.0) + 1e-06)
            scale = jnp.concatenate([table[:, :1], table[:, 64:65]], axis=0)
        ctx, stats = attend(t, 1 - r, scale)
        c_own[t, 0] = ctx
        t_own[t, 0] = stats
        for i in (0, 2, 4, 6):
            m = ring_peers[i]
            send(t_own.at[t, 0], t_all.at[t, n], t_ss.at[t, i], t_rs.at[t, n], ring(m))
            send(c_own.at[t, 0], c_all.at[t, n], c_ss.at[t, i], c_rs.at[t, n], ring(m))
        ctx, stats = attend(t, r, scale)
        c_own[t, 1] = ctx
        t_own[t, 1] = stats
        c_all[t, n] = ctx
        t_all[t, n] = stats
        for i in (1, 3, 5):
            m = ring_peers[i]
            send(t_own.at[t, 1], t_all.at[t, n], t_ss.at[t, i], t_rs.at[t, n], ring(m))
            send(c_own.at[t, 1], c_all.at[t, n], c_ss.at[t, i], c_rs.at[t, n], ring(m))
        if t == 1:
            for i, p in enumerate(head_peers):
                wait_arrival(g_all.at[0, p], g_ss.at[0, i], g_rs.at[0, p], {"head": p})
            for i in range(8):
                for j in range(4):
                    cols = slice(512 * i + 128 * j, 512 * i + 128 * j + 128)
                    one_col = g_all[0, :, i, j, :]
                    out_att[:, cols] = one_col
                    full[:, cols] = pre[:, cols] + one_col
            for i in range(BEAMS):
                picked[pl.ds(i, 1), :] = full[pl.ds(parents[1, i], 1), :]
            full[...] = picked[...] + tokens[1].astype(jnp.float32)
        for i, m in enumerate(ring_peers):
            wait_arrival(t_all.at[t, m], t_ss.at[t, i], t_rs.at[t, m], ring(m))
            wait_arrival(c_all.at[t, m], c_ss.at[t, i], c_rs.at[t, m], ring(m))
        peak, sums, joined = merge(
            [t_all[t, i] for i in range(8)], [c_all[t, i].astype(jnp.float32) for i in range(8)]
        )
        stats = jnp.where(is_top, peak, pltpu.roll(sums, 4, 1))
        v_own[t] = joined
        m_own[t] = stats
        v_all[t, k] = joined
        m_all[t, k] = stats
        send(m_own.at[t], m_all.at[t, k], m_ss.at[t], m_rs.at[t], partner)
        send(v_own.at[t], v_all.at[t, k], v_ss.at[t], v_rs.at[t], partner)
        wait_arrival(m_all.at[t, other], m_ss.at[t], m_rs.at[t], partner)
        wait_arrival(v_all.at[t, other], v_ss.at[t], v_rs.at[t], partner)
        peak, sums, joined = merge([m_all[t, 0], m_all[t, 1]], [v_all[t, 0], v_all[t, 1]])
        context = (joined / spread_rows(sums)).astype(jnp.bfloat16)
        partial = jnp.dot(context, wo[...], preferred_element_type=jnp.float32)
        for j in range(4):
            p_own[t, :, j, :] = partial[:, 128 * j:128 * j + 128]
        p_all[t, c] = p_own[t, c]
        for i, p in enumerate(head_peers):
            send(p_own.at[t, p], p_all.at[t, c], p_ss.at[t, i], p_rs.at[t, c], {"head": p})
        for i, p in enumerate(head_peers):
            wait_arrival(p_all.at[t, p], p_ss.at[t, i], p_rs.at[t, p], {"head": p})
        row = p_all[t, 0]
        for i in range(1, HEAD):
            row += p_all[t, i]
        f_own[t] = row
        f_all[t, s] = row
        if t == 0:
            for i, p in enumerate(head_peers):
                send(f_own.at[t], l_all.at[c], l_ss.at[i], l_rs.at[c], {"head": p})
            l_all[c] = row
        for i, p in enumerate(seq_peers):
            send(f_own.at[t], f_all.at[t, s], f_ss.at[t, i], f_rs.at[t, s], {"seq": p})
        if t == 0:
            for i, p in enumerate(head_peers):
                wait_arrival(l_all.at[p], l_ss.at[i], l_rs.at[p], {"head": p})
    for i, p in enumerate(seq_peers):
        wait_arrival(f_all.at[1, p], f_ss.at[1, i], f_rs.at[1, p], {"seq": p})
    for i, p in enumerate(head_peers):
        send(f_all.at[1], g_all.at[1, c], g_ss.at[1, i], g_rs.at[1, c], {"head": p})
    g_all[1, c] = f_all[1]
    for i, p in enumerate(head_peers):
        wait_arrival(g_all.at[1, p], g_ss.at[1, i], g_rs.at[1, p], {"head": p})
    for i in range(8):
        for j in range(4):
            cols = slice(512 * i + 128 * j, 512 * i + 128 * j + 128)
            one_col = g_all[1, :, i, j, :]
            out_state[:, cols] = full[:, cols] + one_col
            out_att[:, cols] = out_att[:, cols] + one_col
    for copy in sent:
        copy.wait_send()


def on_device(
    enc_out, enc_gain, key_weight, value_weight, query_weight, out_weight,
    dec_gain, beam_state, parents, token_embed,
):
    vmem = pl.BlockSpec(memory_space=pltpu.VMEM)
    f32, bf16 = jnp.float32, jnp.bfloat16
    dma = pltpu.SemaphoreType.DMA
    rows = jax.ShapeDtypeStruct((BEAMS, 4096), f32)

    def pair(*shape):
        return [dma(shape), dma(shape)]

    return pl.pallas_call(
        kernel,
        out_shape=(rows, rows),
        in_specs=[vmem] * 8 + [pl.BlockSpec(memory_space=pltpu.SMEM), vmem],
        out_specs=(vmem, vmem),
        scratch_shapes=[
            pltpu.VMEM((HEAD, 512, 256), bf16),
            pltpu.VMEM((512, 4096), bf16),
            pltpu.VMEM((4, 4096, 256), bf16),
            pltpu.VMEM((4, 512, 256), bf16),
            pltpu.VMEM((BEAMS, 4096), f32),
            pltpu.VMEM((BEAMS, 512), f32),
            pltpu.VMEM((BEAMS, 4096), f32),
            pltpu.VMEM((BEAMS, 512), f32),
            pltpu.VMEM((BEAMS, 4096), f32),
            pltpu.VMEM((STEPS, BEAMS, 256), f32),
            pltpu.VMEM((STEPS, 8, BEAMS, 256), f32),
            pltpu.VMEM((STEPS, 2, BEAMS, 256), f32),
            pltpu.VMEM((STEPS, 2, 2, BEAMS, 256), f32),
            pltpu.VMEM((8, 128), f32),
            pltpu.VMEM((8, 8, 128), f32),
            pltpu.VMEM((8, 128), f32),
            pltpu.VMEM((2, 8, 128), f32),
            pltpu.VMEM((STEPS, 2, BEAMS, 256), bf16),
            pltpu.VMEM((STEPS, 8, BEAMS, 256), bf16),
            pltpu.VMEM((STEPS, 2, 8, 128), f32),
            pltpu.VMEM((STEPS, 8, 8, 128), f32),
            pltpu.VMEM((STEPS, 8, 128), f32),
            pltpu.VMEM((STEPS, 2, 8, 128), f32),
            pltpu.VMEM((STEPS, BEAMS, 256), f32),
            pltpu.VMEM((STEPS, 2, BEAMS, 256), f32),
            pltpu.VMEM((STEPS, BEAMS, 4, 128), f32),
            pltpu.VMEM((STEPS, HEAD, 4, 128), f32),
            pltpu.VMEM((STEPS, 4, 128), f32),
            pltpu.VMEM((STEPS, SEQ, 4, 128), f32),
            pltpu.VMEM((BEAMS, 4, 128), f32),
            pltpu.VMEM((STEPS, BEAMS, 8, 4, 128), f32),
            dma((3,)),
            *pair(9), *pair(8, 2), *pair(8, 2), *pair(8, 4), *pair(3), *pair(4, 2), *pair(4, 2),
            *pair(STEPS, 8), *pair(STEPS), *pair(8), *pair(1), *pair(STEPS, 8), *pair(STEPS, 8),
            *pair(STEPS), *pair(STEPS), *pair(STEPS, HEAD), *pair(STEPS, SEQ), *pair(HEAD), *pair(STEPS, HEAD),
        ],
        compiler_params=pltpu.CompilerParams(collective_id=1, has_side_effects=True),
        name="beam_decode",
    )(
        enc_out, enc_gain.reshape(1, 4096), key_weight, value_weight, query_weight, out_weight,
        dec_gain.reshape(1, 4096), beam_state, parents, token_embed,
    )


def solution(mesh):
    placed = (
        P(("src", "seq"), "head"),
        P(),
        P("seq", "head"),
        P("seq", "head"),
        P("seq", "head"),
        P("head", "seq"),
        P(),
        P("src", None),
        P("src", None),
        P("src", None, None),
    )
    return jax.shard_map(
        on_device,
        mesh=mesh,
        in_specs=placed,
        out_specs=(P("src", None), P("src", None)),
        check_vma=False,
    )
```

time: 189 us -> 159 us (0.84)
  Pallas kernels: 180 us -> 155 us
  local copies, waits for them, and re-layouts: 7.02 us -> 2.42 us
    pallas_call x2 -> x1, Pallas kernels: 180 us -> 155 us  [on_device(): pl.pallas_call(kernel, out_shape=(rows, rows), in_specs=[vmem] * 8 + [pl....]
    reshape x5 -> x0, local copies, waits for them, and re-layouts: 7.01 us -> none  [the longest x2 2.61 us: on_device(): return (state.reshape(BEAMS, 4096), attended.reshape(BEAMS, 4096))]
    unnamed x4, local copies, waits for them, and re-layouts: 0.01 us -> 2.42 us
where the time goes in v3:
time: 159 us; the launch traced here: 158 us
  Pallas kernels  155 us (97%)
  local copies, waits for them, and re-layouts  2.42 us (2%)
    pallas_call x1, Pallas kernels, on_device(): pl.pallas_call(kernel, out_shape=(rows, rows), in_specs=[vmem] * 8 + [pl....  155 us

profile of v3, /device:TPU:6, one launch (start us, length us, event | category | flops | bytes accessed | tf_op | source)
XLA Modules:
  0.0 158.2 jit_solution(16199870580994112310)
XLA Ops:
  0.6 155.2 %beam_decode.1 = (f32[16,4096]{1,0:T(8,128)}, f32[16,4096]{1,0:T(8,128)}) custom-call(bf16[1024,256]{1,0:T(8,128)(2,1)} %enc.1, f32[1,4096]{1,0:T(1,128)} %bitcast.2, bf16[512,256]{1,0:T(8,128)(2,1)} %wk.1, bf16[512,256]{1,0:T(8,128)(2,1)} %wv.1, bf16[512,256]{1,0:T(8,128)(2,1)} %wq.1, bf16[256,512]{1,0:T(8,128)(2,1)} %wo.1, f32[1,4096]{1,0:T(1,128)} %bitcast.3, ...), custom_call_target="tpu_custom_call" | custom-call | tf_op jit(solution)/shard_map/beam_decode/pallas_call | solution.py:478
  155.8 0.0 copy-start
  155.8 1.7 %copy.14 = f32[16,4096]{1,0:T(8,128)} copy(f32[16,4096]{1,0:T(8,128)} %get-tuple-element.4) | data formatting | bytes 524288
  157.5 0.0 copy-done
  157.5 0.7 copy.15
Async XLA Ops:
  155.8 1.7 %copy-start = (f32[16,4096]{1,0:T(8,128)S(1)}, f32[16,4096]{1,0:T(8,128)}, u32[]{:S(2)}) copy-start(f32[16,4096]{1,0:T(8,128)} %get-tuple-element.5) | copy-start | bytes 786436

commit v4 on v3

--- a/solution.py
+++ b/solution.py
@@ -53,7 +53,7 @@
 
 def kernel(
     enc, enc_gain, wk, wv, wq, wo, gain, first, parents, tokens,
-    out_state, out_att,
+    out_pre, out_first, out_second,
     ebuf, nbuf, wbuf, kv,
     pre, part, picked, local_rows, full,
     q_own, q_all, u_own, u_all, z_own, z_all, zz_own, zz_all, c_own, c_all, t_own, t_all, m_own, m_all, v_own, v_all,
@@ -87,20 +87,26 @@
         m = nodes(q)
         return wbuf.at[2 * lax.rem(m, 2) + mat, rows_of(m, quarters[j], k), :]
 
+    def shard(mat):
+        at = pl.ds(pl.multiple_of(s * 512, 512), 512)
+        return wbuf.at[2 * r + mat, at, :]
+
+    def shard_both(core):
+        at = pl.ds(pl.multiple_of((lax.div(n, 2) * 2 + core) * 512, 512), 512)
+        return wbuf.at[pl.ds(2 * r, 2), at, :]
+
     def local(src, dst, i):
         copy = pltpu.make_async_copy(src, dst, own_sem.at[i])
         copy.start()
         return copy
 
-    mine = pl.ds(pl.multiple_of(y * 128, 128), 128)
     near = pl.ds(pl.multiple_of(r * 512, 512), 512)
     far = pl.ds(pl.multiple_of(512 - r * 512, 512), 512)
     locals_ = [
-        local(wk.at[mine, :], one(0, 0, 0), 0),
-        local(wv.at[mine, :], one(0, 0, 1), 1),
+        local(wk, shard(0), 0),
+        local(wv, shard(1), 1),
         local(enc.at[near, :], ebuf.at[c], 2),
     ]
-
     seq_peers = [lax.rem(s + i, SEQ) for i in range(1, SEQ)]
     head_peers = [lax.rem(c + i, HEAD) for i in range(1, HEAD)]
     ring_peers = [lax.rem(n + i, 8) for i in range(1, 8)]
@@ -123,41 +129,36 @@
     sent = []
     send = functools.partial(start_send, sent)
 
-    def z_on(q):
+    def z_on(q, mat):
         off = OFFSETS[q]
-        if off <= 0 and off > -3:
-            t = BY_OFFSET[off - 1]
-            send(both(q, 0, k), both(q, 0, k), wz_ss.at[t], wz_rs.at[t], right)
-        if off >= 0 and off < 3:
-            t = BY_OFFSET[off + 1]
-            send(both(q, 0, k), both(q, 0, k), wz_ss.at[t], wz_rs.at[t], left)
-        if off == -3:
-            send(one(q, 0, 0), one(q, 0, 0), wz_ss.at[7], wz_rs.at[7], right)
-        if off == 3:
-            send(one(q, 0, 1), one(q, 0, 1), wz_ss.at[8], wz_rs.at[8], left)
-
-    def z_in(q):
-        off = OFFSETS[q]
-        if off == 4:
-            wait_arrival(one(q, 0, 0), wz_ss.at[7], wz_rs.at[7], right)
-            wait_arrival(one(q, 0, 1), wz_ss.at[8], wz_rs.at[8], left)
-        else:
-            wait_arrival(both(q, 0, k), wz_ss.at[q], wz_rs.at[q], right)
+        if -3 < off <= 0 or (off == -3 and mat == 0):
+            t = 7 if off == -3 else BY_OFFSET[off - 1]
+            send(one(q, 0, mat), one(q, 0, mat), wz_ss.at[t, mat], wz_rs.at[t, mat], right)
+        if 0 <= off < 3 or (off == 3 and mat == 1):
+            t = 7 if off == 3 else BY_OFFSET[off + 1]
+            send(one(q, 0, mat), one(q, 0, mat), wz_ss.at[t, mat], wz_rs.at[t, mat], left)
+
+    def z_step(q, mat):
+        wait_arrival(one(q, 0, mat), wz_ss.at[q, mat], wz_rs.at[q, mat], right)
+        z_on(q, mat)
+        send(one(q, 0, mat), one(q, 0, mat), wy_ss.at[q, mat, 0], wy_rs.at[q, mat, 0], up)
+        send(one(q, 0, mat), one(q, 0, mat), wy_ss.at[q, mat, 1], wy_rs.at[q, mat, 1], down)
+        if mat == 1:
+            cross(q, 0)
 
     def cross(q, j):
         send(both(q, j, k), both(q, j, k), wc_ss.at[q, j], wc_rs.at[q, j], partner)
 
-    def y_out(q):
-        send(both(q, 0, k), both(q, 0, k), wy_ss.at[q, 0], wy_rs.at[q, 0], up)
-        send(both(q, 0, k), both(q, 0, k), wy_ss.at[q, 1], wy_rs.at[q, 1], down)
-        cross(q, 0)
-
     def y_relay(q):
-        wait_arrival(both(q, 1, k), wy_ss.at[q, 0], wy_rs.at[q, 0], up)
+        wait_arrival(one(q, 1, 0), wy_ss.at[q, 0, 0], wy_rs.at[q, 0, 0], up)
         send(one(q, 1, 0), one(q, 1, 0), wh_ss.at[q, 0], wh_rs.at[q, 0], up)
+        wait_arrival(one(q, 2, 1), wy_ss.at[q, 1, 1], wy_rs.at[q, 1, 1], down)
+        send(one(q, 2, 1), one(q, 2, 1), wh_ss.at[q, 1], wh_rs.at[q, 1], down)
+
+    def y_cross(q):
+        wait_arrival(one(q, 1, 1), wy_ss.at[q, 1, 0], wy_rs.at[q, 1, 0], up)
         cross(q, 1)
-        wait_arrival(both(q, 2, k), wy_ss.at[q, 1], wy_rs.at[q, 1], down)
-        send(one(q, 2, 1), one(q, 2, 1), wh_ss.at[q, 1], wh_rs.at[q, 1], down)
+        wait_arrival(one(q, 2, 0), wy_ss.at[q, 0, 1], wy_rs.at[q, 0, 1], down)
         cross(q, 2)
 
     def y_last(q):
@@ -166,28 +167,41 @@
         cross(q, 3)
 
     piece_z = [zl, sibling, opposite, lax.rem(sibling + 2, 4)]
-
-    def piece(p, xs):
-        return ebuf.at[piece_z[p] * 4 + xs]
-
     xs = [x, lax.rem(x + 3, 4), lax.rem(x + 1, 4), lax.rem(x + 2, 4)]
-    top_half, low_half = pl.ds(0, 256), pl.ds(256, 256)
-
-    def x_out(p):
-        send(piece(p, x), piece(p, x), ex_ss.at[p, 0], ex_rs.at[p, 0], east)
-        send(piece(p, x), piece(p, x), ex_ss.at[p, 1], ex_rs.at[p, 1], west)
+
+    def half(p, xs_, i):
+        return ebuf.at[piece_z[p] * 4 + xs_, pl.ds(256 * i, 256), :]
+
+    def own_half(at, i):
+        return enc.at[pl.ds(pl.multiple_of(at + 256 * i, 256), 256), :]
+
+    def e_near(i):
+        send(own_half(r * 512, i), half(0, x, i), ez_ss.at[0, i], ez_rs.at[0, i], {"head": sibling * 4 + x})
+
+    def e_far(i):
+        send(own_half(512 - r * 512, i), half(0, x, i), ez_ss.at[1, i], ez_rs.at[1, i], {"head": opposite * 4 + x})
+
+    def e_step(p, i):
+        wait_arrival(half(p, x, i), ez_ss.at[p - 1, i], ez_rs.at[p - 1, i], east)
+        if p == 2:
+            send(half(2, x, i), half(2, x, i), ez_ss.at[2, i], ez_rs.at[2, i], {"head": sibling * 4 + x})
+        x_out(p, i)
+
+    def x_out(p, i):
+        for d, where in ((0, east), (1, west)):
+            send(half(p, x, i), half(p, x, i), ex_ss.at[p, i, d], ex_rs.at[p, i, d], where)
 
     def x_relay(p):
-        wait_arrival(piece(p, xs[1]), ex_ss.at[p, 0], ex_rs.at[p, 0], east)
-        part = piece(p, xs[1]).at[top_half, :]
-        send(part, part, eh_ss.at[p, 0], eh_rs.at[p, 0], east)
-        wait_arrival(piece(p, xs[2]), ex_ss.at[p, 1], ex_rs.at[p, 1], west)
-        part = piece(p, xs[2]).at[low_half, :]
-        send(part, part, eh_ss.at[p, 1], eh_rs.at[p, 1], west)
+        wait_arrival(half(p, xs[1], 0), ex_ss.at[p, 0, 0], ex_rs.at[p, 0, 0], east)
+        send(half(p, xs[1], 0), half(p, xs[1], 0), eh_ss.at[p, 0], eh_rs.at[p, 0], east)
+        wait_arrival(half(p, xs[2], 1), ex_ss.at[p, 1, 1], ex_rs.at[p, 1, 1], west)
+        send(half(p, xs[2], 1), half(p, xs[2], 1), eh_ss.at[p, 1], eh_rs.at[p, 1], west)
 
     def x_last(p):
-        wait_arrival(piece(p, xs[3]).at[top_half, :], eh_ss.at[p, 0], eh_rs.at[p, 0], east)
-        wait_arrival(piece(p, xs[3]).at[low_half, :], eh_ss.at[p, 1], eh_rs.at[p, 1], west)
+        wait_arrival(half(p, xs[1], 1), ex_ss.at[p, 1, 0], ex_rs.at[p, 1, 0], east)
+        wait_arrival(half(p, xs[2], 0), ex_ss.at[p, 0, 1], ex_rs.at[p, 0, 1], west)
+        wait_arrival(half(p, xs[3], 0), eh_ss.at[p, 0], eh_rs.at[p, 0], east)
+        wait_arrival(half(p, xs[3], 1), eh_ss.at[p, 1], eh_rs.at[p, 1], west)
 
     col_head = lax.broadcasted_iota(jnp.int32, (BEAMS, 256), 1) // HEAD_DIM
     lane = lax.broadcasted_iota(jnp.int32, (8, 128), 1)
@@ -205,6 +219,20 @@
             halves.append(scale)
         return jnp.concatenate(halves, axis=0)
 
+    row_of = lax.broadcasted_iota(jnp.int32, (8, 128), 0)
+
+    def swap_rows(tile, step):
+        return jnp.where(
+            lax.rem(lax.div(row_of, step), 2) == 0, pltpu.roll(tile, 8 - step, 0), pltpu.roll(tile, step, 0)
+        )
+
+    def fold(tile):
+        turned = swap_rows(swap_rows(pltpu.roll(tile, 4, 0), 2), 1)
+        return jnp.sum(pltpu.roll(turned, 0, 1, stride=16, stride_axis=0), axis=0, keepdims=True)
+
+    def unfold(row):
+        return pltpu.roll(jnp.broadcast_to(row, (8, 128)), 16, 1, stride=16, stride_axis=0)
+
     def merge(stats, parts):
         peak = functools.reduce(jnp.maximum, stats)
         factors = [jnp.exp(one - peak) for one in stats]
@@ -217,7 +245,8 @@
         return peak, sums, joined
 
     def query_out(t):
-        for i, m in enumerate(ring_peers):
+        for i in (3, 2, 4, 1, 5, 0, 6):
+            m = ring_peers[i]
             if t == 1:
                 send(z_own, z_all.at[n], z_ss.at[i], z_rs.at[n], ring(m))
             send(q_own.at[t], q_all.at[t, n], q_ss.at[t, i], q_rs.at[t, n], ring(m))
@@ -268,11 +297,15 @@
                 stats = jnp.where(lane == 8 * half + 4 + h, total[at:at + 8], stats)
         return ctx.astype(jnp.bfloat16), stats
 
-    z_on(0)
-    send(enc.at[near, :], ebuf.at[c], ez_ss.at[0], ez_rs.at[0], {"head": sibling * 4 + x})
-    send(enc.at[far, :], ebuf.at[c], ez_ss.at[1], ez_rs.at[1], {"head": opposite * 4 + x})
-    y_out(0)
-    x_out(0)
+    z_on(0, 0)
+    z_on(0, 1)
+    e_near(0)
+    e_far(0)
+    e_near(1)
+    e_far(1)
+    x_out(0, 0)
+    x_out(0, 1)
+    send(shard_both(k), shard_both(k), wc_ss.at[0, 0], wc_rs.at[0, 0], partner)
 
     for i in range(BEAMS):
         picked[pl.ds(i, 1), :] = first[pl.ds(parents[0, i], 1), :]
@@ -284,47 +317,55 @@
     q_all[0, n] = q_own[0]
     query_out(0)
 
-    def weights_round(qs):
-        for q in qs:
-            z_in(q)
-            z_on(q)
-            y_out(q)
-
-    weights_round([1, 2])
-    y_relay(0)
+    z_step(1, 0)
+    z_step(2, 0)
+    z_step(1, 1)
+    z_step(2, 1)
     x_relay(0)
-    wait_arrival(piece(1, x), ez_ss.at[0], ez_rs.at[0], east)
-    x_out(1)
-    wait_arrival(piece(2, x), ez_ss.at[1], ez_rs.at[1], east)
-    send(piece(2, x), piece(2, x), ez_ss.at[2], ez_rs.at[2], {"head": sibling * 4 + x})
-    x_out(2)
-    weights_round([3, 4])
+    e_step(1, 0)
+    e_step(1, 1)
+    z_step(3, 0)
+    z_step(4, 0)
+    z_step(3, 1)
+    z_step(4, 1)
+    e_step(2, 0)
+    e_step(2, 1)
     y_relay(1)
     y_relay(2)
-    y_last(0)
     x_relay(1)
+    z_step(5, 0)
+    z_step(6, 0)
+    z_step(5, 1)
+    z_step(6, 1)
     x_last(0)
-    weights_round([5, 6])
-    wait_arrival(piece(3, x), ez_ss.at[2], ez_rs.at[2], east)
-    x_out(3)
     y_relay(3)
     y_relay(4)
+    y_cross(1)
+    y_cross(2)
     x_relay(2)
+    x_last(1)
+    e_step(3, 0)
+    e_step(3, 1)
+    z_step(7, 0)
+    z_step(7, 1)
     y_last(1)
     y_last(2)
-    x_last(1)
-    weights_round([7])
     query_swap(0)
     y_relay(5)
     y_relay(6)
+    y_cross(3)
+    y_cross(4)
     x_relay(3)
     y_last(3)
     y_last(4)
     x_last(2)
     y_relay(7)
+    y_cross(5)
+    y_cross(6)
     y_last(5)
     y_last(6)
     x_last(3)
+    y_cross(7)
     y_last(7)
 
     @pl.loop(0, 8)
@@ -341,7 +382,8 @@
             block = ebuf[f, at, :].astype(jnp.float32) * scale * enc_gain[:, cols]
             nbuf[at, cols] = block.astype(jnp.bfloat16)
 
-    for q in range(8):
+    wait_arrival(shard_both(other), wc_ss.at[0, 0], wc_rs.at[0, 0], partner)
+    for q in range(1, 8):
         for j in range(4):
             wait_arrival(both(q, j, other), wc_ss.at[q, j], wc_rs.at[q, j], partner)
 
@@ -359,7 +401,9 @@
                 local_rows[pl.ds(i, 1), :] = part[pl.ds(parents[1, i], 1), :]
             rows = local_rows[...] + tokens[1, :, feats].astype(jnp.float32)
             squares = jnp.sum(rows * rows, axis=-1, keepdims=True)
-            z_own[...] = jnp.where(lane < 64, squares[:8], squares[8:])
+            z_own[...] = fold(
+                jnp.where(lane == 0, squares[:8], jnp.where(lane == 1, squares[8:], 0.0))
+            )
             z_all[n] = z_own[...]
             scaled = rows * gain[:, feats]
             high = scaled.astype(jnp.bfloat16)
@@ -377,24 +421,18 @@
             g_all[0, c] = f_all[0]
         query_in(t)
         if t == 1:
-            table = lax.rsqrt((zz_all[0] + zz_all[1]) * (1.0 / 4096.0) + 1e-06)
-            scale = jnp.concatenate([table[:, :1], table[:, 64:65]], axis=0)
-        ctx, stats = attend(t, 1 - r, scale)
-        c_own[t, 0] = ctx
-        t_own[t, 0] = stats
-        for i in (0, 2, 4, 6):
-            m = ring_peers[i]
-            send(t_own.at[t, 0], t_all.at[t, n], t_ss.at[t, i], t_rs.at[t, n], ring(m))
-            send(c_own.at[t, 0], c_all.at[t, n], c_ss.at[t, i], c_rs.at[t, n], ring(m))
-        ctx, stats = attend(t, r, scale)
-        c_own[t, 1] = ctx
-        t_own[t, 1] = stats
-        c_all[t, n] = ctx
-        t_all[t, n] = stats
-        for i in (1, 3, 5):
-            m = ring_peers[i]
-            send(t_own.at[t, 1], t_all.at[t, n], t_ss.at[t, i], t_rs.at[t, n], ring(m))
-            send(c_own.at[t, 1], c_all.at[t, n], c_ss.at[t, i], c_rs.at[t, n], ring(m))
+            table = lax.rsqrt(unfold(zz_all[0] + zz_all[1]) * (1.0 / 4096.0) + 1e-06)
+            scale = jnp.concatenate([table[:, :1], table[:, 1:2]], axis=0)
+        for slot, g, order in ((1, r, (3, 1, 5)), (0, 1 - r, (2, 4, 0, 6))):
+            ctx, stats = attend(t, g, scale)
+            c_own[t, slot] = ctx
+            t_own[t, slot] = fold(stats)
+            for i in order:
+                m = ring_peers[i]
+                send(t_own.at[t, slot], t_all.at[t, n], t_ss.at[t, i], t_rs.at[t, n], ring(m))
+                send(c_own.at[t, slot], c_all.at[t, n], c_ss.at[t, i], c_rs.at[t, n], ring(m))
+        c_all[t, n] = c_own[t, 1]
+        t_all[t, n] = t_own[t, 1]
         if t == 1:
             for i, p in enumerate(head_peers):
                 wait_arrival(g_all.at[0, p], g_ss.at[0, i], g_rs.at[0, p], {"head": p})
@@ -402,16 +440,16 @@
                 for j in range(4):
                     cols = slice(512 * i + 128 * j, 512 * i + 128 * j + 128)
                     one_col = g_all[0, :, i, j, :]
-                    out_att[:, cols] = one_col
+                    out_first[:, cols] = one_col
                     full[:, cols] = pre[:, cols] + one_col
             for i in range(BEAMS):
                 picked[pl.ds(i, 1), :] = full[pl.ds(parents[1, i], 1), :]
-            full[...] = picked[...] + tokens[1].astype(jnp.float32)
+            out_pre[...] = picked[...] + tokens[1].astype(jnp.float32)
         for i, m in enumerate(ring_peers):
             wait_arrival(t_all.at[t, m], t_ss.at[t, i], t_rs.at[t, m], ring(m))
             wait_arrival(c_all.at[t, m], c_ss.at[t, i], c_rs.at[t, m], ring(m))
         peak, sums, joined = merge(
-            [t_all[t, i] for i in range(8)], [c_all[t, i].astype(jnp.float32) for i in range(8)]
+            [unfold(t_all[t, i]) for i in range(8)], [c_all[t, i].astype(jnp.float32) for i in range(8)]
         )
         stats = jnp.where(is_top, peak, pltpu.roll(sums, 4, 1))
         v_own[t] = joined
@@ -457,8 +495,7 @@
         for j in range(4):
             cols = slice(512 * i + 128 * j, 512 * i + 128 * j + 128)
             one_col = g_all[1, :, i, j, :]
-            out_state[:, cols] = full[:, cols] + one_col
-            out_att[:, cols] = out_att[:, cols] + one_col
+            out_second[:, cols] = one_col
     for copy in sent:
         copy.wait_send()
 
@@ -475,11 +512,11 @@
     def pair(*shape):
         return [dma(shape), dma(shape)]
 
-    return pl.pallas_call(
+    before, once, twice = pl.pallas_call(
         kernel,
-        out_shape=(rows, rows),
+        out_shape=(rows, rows, rows),
         in_specs=[vmem] * 8 + [pl.BlockSpec(memory_space=pltpu.SMEM), vmem],
-        out_specs=(vmem, vmem),
+        out_specs=(vmem, vmem, vmem),
         scratch_shapes=[
             pltpu.VMEM((HEAD, 512, 256), bf16),
             pltpu.VMEM((512, 4096), bf16),
@@ -494,14 +531,14 @@
             pltpu.VMEM((STEPS, 8, BEAMS, 256), f32),
             pltpu.VMEM((STEPS, 2, BEAMS, 256), f32),
             pltpu.VMEM((STEPS, 2, 2, BEAMS, 256), f32),
-            pltpu.VMEM((8, 128), f32),
-            pltpu.VMEM((8, 8, 128), f32),
-            pltpu.VMEM((8, 128), f32),
-            pltpu.VMEM((2, 8, 128), f32),
+            pltpu.VMEM((1, 128), f32),
+            pltpu.VMEM((8, 1, 128), f32),
+            pltpu.VMEM((1, 128), f32),
+            pltpu.VMEM((2, 1, 128), f32),
             pltpu.VMEM((STEPS, 2, BEAMS, 256), bf16),
             pltpu.VMEM((STEPS, 8, BEAMS, 256), bf16),
-            pltpu.VMEM((STEPS, 2, 8, 128), f32),
-            pltpu.VMEM((STEPS, 8, 8, 128), f32),
+            pltpu.VMEM((STEPS, 2, 1, 128), f32),
+            pltpu.VMEM((STEPS, 8, 1, 128), f32),
             pltpu.VMEM((STEPS, 8, 128), f32),
             pltpu.VMEM((STEPS, 2, 8, 128), f32),
             pltpu.VMEM((STEPS, BEAMS, 256), f32),
@@ -513,7 +550,7 @@
             pltpu.VMEM((BEAMS, 4, 128), f32),
             pltpu.VMEM((STEPS, BEAMS, 8, 4, 128), f32),
             dma((3,)),
-            *pair(9), *pair(8, 2), *pair(8, 2), *pair(8, 4), *pair(3), *pair(4, 2), *pair(4, 2),
+            *pair(8, 2), *pair(8, 2, 2), *pair(8, 2), *pair(8, 4), *pair(3, 2), *pair(4, 2, 2), *pair(4, 2),
             *pair(STEPS, 8), *pair(STEPS), *pair(8), *pair(1), *pair(STEPS, 8), *pair(STEPS, 8),
             *pair(STEPS), *pair(STEPS), *pair(STEPS, HEAD), *pair(STEPS, SEQ), *pair(HEAD), *pair(STEPS, HEAD),
         ],
@@ -523,6 +560,7 @@
         enc_out, enc_gain.reshape(1, 4096), key_weight, value_weight, query_weight, out_weight,
         dec_gain.reshape(1, 4096), beam_state, parents, token_embed,
     )
+    return before + twice, once + twice
 
 
 def solution(mesh):

time: 159 us -> 150 us (0.943)
  Pallas kernels: 155 us -> 147 us
  local copies, waits for them, and re-layouts: 2.42 us -> 0 us
  other arithmetic: 0 us -> 1.94 us
    pallas_call x1, Pallas kernels: 155 us -> 147 us  [on_device(): pl.pallas_call(kernel, out_shape=(rows, rows, rows), in_specs=[vmem] * 8...]
    unnamed x4 -> x0, local copies, waits for them, and re-layouts: 2.42 us -> none
    add x0 -> x1, other arithmetic: none -> 1.94 us  [on_device(): return (before + twice, once + twice)]
where the time goes in v4:
time: 150 us; the launch traced here: 149 us
  Pallas kernels  147 us (98%)
  other arithmetic  1.94 us (1%)
    pallas_call x1, Pallas kernels, on_device(): pl.pallas_call(kernel, out_shape=(rows, rows, rows), in_specs=[vmem] * 8...  147 us

profile of v4, /device:TPU:6, one launch (start us, length us, event | category | flops | bytes accessed | tf_op | source)
XLA Modules:
  0.0 149.4 jit_solution(16789692597338241027)
XLA Ops:
  0.6 146.8 %beam_decode.1 = (f32[16,4096]{1,0:T(8,128)}, f32[16,4096]{1,0:T(8,128)}, f32[16,4096]{1,0:T(8,128)}) custom-call(bf16[1024,256]{1,0:T(8,128)(2,1)} %enc.1, f32[1,4096]{1,0:T(1,128)} %bitcast.2, bf16[512,256]{1,0:T(8,128)(2,1)} %wk.1, bf16[512,256]{1,0:T(8,128)(2,1)} %wv.1, bf16[512,256]{1,0:T(8,128)(2,1)} %wq.1, bf16[256,512]{1,0:T(8,128)(2,1)} %wo.1, ...), custom_call_target="tpu_custom_call" | custom-call | tf_op jit(solution)/shard_map/beam_decode/pallas_call | solution.py:515
  147.4 1.9 %fusion = (f32[16,4096]{1,0:T(8,128)}, f32[16,4096]{1,0:T(8,128)}) fusion(f32[16,4096]{1,0:T(8,128)} %get-tuple-element.7, f32[16,4096]{1,0:T(8,128)} %get-tuple-element.6, f32[16,4096]{1,0:T(8,128)} %get-tuple-element.5), kind=kLoop, calls=%fused_computation | loop fusion | flops 131072 | bytes 1310720 | tf_op jit(solution)/shard_map/add | solution.py:563

commit v5 on v4

--- a/solution.py
+++ b/solution.py
@@ -52,13 +52,14 @@
 
 
 def kernel(
-    enc, enc_gain, wk, wv, wq, wo, gain, first, parents, tokens,
-    out_pre, out_first, out_second,
+    enc, enc_gain_in, wk, wv, wq_in, wo_in, gain_in, first_in, parents, tokens_in,
+    pre_out, first_out, second_out,
+    enc_gain, wq, wo, gain, first, tokens, out_pre, out_first, out_second,
     ebuf, nbuf, wbuf, kv,
     pre, part, picked, local_rows, full,
     q_own, q_all, u_own, u_all, z_own, z_all, zz_own, zz_all, c_own, c_all, t_own, t_all, m_own, m_all, v_own, v_all,
     p_own, p_all, f_own, f_all, l_all, g_all,
-    own_sem, wz_ss, wz_rs, wy_ss, wy_rs, wh_ss, wh_rs, wc_ss, wc_rs, ez_ss, ez_rs, ex_ss, ex_rs, eh_ss, eh_rs,
+    own_sem, in_sem, out_sem, wz_ss, wz_rs, wy_ss, wy_rs, wh_ss, wh_rs, wc_ss, wc_rs, ez_ss, ez_rs, ex_ss, ex_rs, eh_ss, eh_rs,
     q_ss, q_rs, u_ss, u_rs, z_ss, z_rs, zz_ss, zz_rs, c_ss, c_rs, t_ss, t_rs, m_ss, m_rs, v_ss, v_rs,
     p_ss, p_rs, f_ss, f_rs, l_ss, l_rs, g_ss, g_rs,
 ):
@@ -102,26 +103,36 @@
 
     near = pl.ds(pl.multiple_of(r * 512, 512), 512)
     far = pl.ds(pl.multiple_of(512 - r * 512, 512), 512)
+    seq_peers = [lax.rem(s + i, SEQ) for i in range(1, SEQ)]
+    head_peers = [lax.rem(c + i, HEAD) for i in range(1, HEAD)]
+    ring_peers = [lax.rem(n + i, 8) for i in range(1, 8)]
+    other = 1 - k
+    feats = pl.ds(pl.multiple_of(s * 512, 512), 512)
+
+    def ring(m):
+        return node_id(m, k, b, x)
+
+    barrier = pltpu.get_barrier_semaphore()
+    greet = [up, down, east, west, partner, right, left]
+    greet += [{"head": sibling * 4 + x}, {"head": opposite * 4 + x}]
+    for where in greet:
+        pl.semaphore_signal(barrier, inc=1, device_id=where, device_id_type=MESH)
     locals_ = [
         local(wk, shard(0), 0),
         local(wv, shard(1), 1),
         local(enc.at[near, :], ebuf.at[c], 2),
     ]
-    seq_peers = [lax.rem(s + i, SEQ) for i in range(1, SEQ)]
-    head_peers = [lax.rem(c + i, HEAD) for i in range(1, HEAD)]
-    ring_peers = [lax.rem(n + i, 8) for i in range(1, 8)]
-    other = 1 - k
-    feats = pl.ds(pl.multiple_of(s * 512, 512), 512)
-
-    def ring(m):
-        return node_id(m, k, b, x)
-
-    barrier = pltpu.get_barrier_semaphore()
-    greet = [up, down]
-    greet += [{"seq": p} for p in seq_peers] + [{"head": p} for p in head_peers]
-    greet += [ring(m) for m in ring_peers]
-    for where in greet:
-        pl.semaphore_signal(barrier, inc=1, device_id=where, device_id_type=MESH)
+    loads = [
+        pltpu.make_async_copy(src, dst, in_sem.at[i])
+        for i, (src, dst) in enumerate(
+            (
+                (first_in, first), (tokens_in, tokens), (gain_in, gain), (wq_in, wq),
+                (enc_gain_in, enc_gain), (wo_in, wo),
+            )
+        )
+    ]
+    for copy in loads:
+        copy.start()
     for copy in locals_:
         copy.wait()
     pl.semaphore_wait(barrier, len(greet))
@@ -176,7 +187,7 @@
         return enc.at[pl.ds(pl.multiple_of(at + 256 * i, 256), 256), :]
 
     def e_near(i):
-        send(own_half(r * 512, i), half(0, x, i), ez_ss.at[0, i], ez_rs.at[0, i], {"head": sibling * 4 + x})
+        send(half(0, x, i), half(0, x, i), ez_ss.at[0, i], ez_rs.at[0, i], {"head": sibling * 4 + x})
 
     def e_far(i):
         send(own_half(512 - r * 512, i), half(0, x, i), ez_ss.at[1, i], ez_rs.at[1, i], {"head": opposite * 4 + x})
@@ -307,6 +318,8 @@
     x_out(0, 1)
     send(shard_both(k), shard_both(k), wc_ss.at[0, 0], wc_rs.at[0, 0], partner)
 
+    for copy in loads:
+        copy.wait()
     for i in range(BEAMS):
         picked[pl.ds(i, 1), :] = first[pl.ds(parents[0, i], 1), :]
     start = picked[...] + tokens[0].astype(jnp.float32)
@@ -315,7 +328,6 @@
     picked[...] = start * lax.rsqrt(mean + 1e-06) * gain[...]
     q_own[0] = jnp.dot(picked[:, feats].astype(jnp.bfloat16), wq[...], preferred_element_type=jnp.float32)
     q_all[0, n] = q_own[0]
-    query_out(0)
 
     z_step(1, 0)
     z_step(2, 0)
@@ -348,6 +360,7 @@
     e_step(3, 1)
     z_step(7, 0)
     z_step(7, 1)
+    query_out(0)
     y_last(1)
     y_last(2)
     query_swap(0)
@@ -445,6 +458,12 @@
             for i in range(BEAMS):
                 picked[pl.ds(i, 1), :] = full[pl.ds(parents[1, i], 1), :]
             out_pre[...] = picked[...] + tokens[1].astype(jnp.float32)
+            stores = [
+                pltpu.make_async_copy(out_pre, pre_out, out_sem.at[0]),
+                pltpu.make_async_copy(out_first, first_out, out_sem.at[1]),
+            ]
+            for copy in stores:
+                copy.start()
         for i, m in enumerate(ring_peers):
             wait_arrival(t_all.at[t, m], t_ss.at[t, i], t_rs.at[t, m], ring(m))
             wait_arrival(c_all.at[t, m], c_ss.at[t, i], c_rs.at[t, m], ring(m))
@@ -496,15 +515,19 @@
             cols = slice(512 * i + 128 * j, 512 * i + 128 * j + 128)
             one_col = g_all[1, :, i, j, :]
             out_second[:, cols] = one_col
+    stores.append(pltpu.make_async_copy(out_second, second_out, out_sem.at[2]))
+    stores[2].start()
     for copy in sent:
         copy.wait_send()
+    for copy in stores:
+        copy.wait()
 
 
 def on_device(
     enc_out, enc_gain, key_weight, value_weight, query_weight, out_weight,
     dec_gain, beam_state, parents, token_embed,
 ):
-    vmem = pl.BlockSpec(memory_space=pltpu.VMEM)
+    anywhere = pl.BlockSpec(memory_space=pl.ANY)
     f32, bf16 = jnp.float32, jnp.bfloat16
     dma = pltpu.SemaphoreType.DMA
     rows = jax.ShapeDtypeStruct((BEAMS, 4096), f32)
@@ -515,9 +538,18 @@
     before, once, twice = pl.pallas_call(
         kernel,
         out_shape=(rows, rows, rows),
-        in_specs=[vmem] * 8 + [pl.BlockSpec(memory_space=pltpu.SMEM), vmem],
-        out_specs=(vmem, vmem, vmem),
+        in_specs=[anywhere] * 8 + [pl.BlockSpec(memory_space=pltpu.SMEM), anywhere],
+        out_specs=(anywhere, anywhere, anywhere),
         scratch_shapes=[
+            pltpu.VMEM((1, 4096), f32),
+            pltpu.VMEM((512, 256), bf16),
+            pltpu.VMEM((256, 512), bf16),
+            pltpu.VMEM((1, 4096), f32),
+            pltpu.VMEM((BEAMS, 4096), f32),
+            pltpu.VMEM((STEPS, BEAMS, 4096), bf16),
+            pltpu.VMEM((BEAMS, 4096), f32),
+            pltpu.VMEM((BEAMS, 4096), f32),
+            pltpu.VMEM((BEAMS, 4096), f32),
             pltpu.VMEM((HEAD, 512, 256), bf16),
             pltpu.VMEM((512, 4096), bf16),
             pltpu.VMEM((4, 4096, 256), bf16),
@@ -549,7 +581,7 @@
             pltpu.VMEM((STEPS, SEQ, 4, 128), f32),
             pltpu.VMEM((BEAMS, 4, 128), f32),
             pltpu.VMEM((STEPS, BEAMS, 8, 4, 128), f32),
-            dma((3,)),
+            dma((3,)), dma((6,)), dma((3,)),
             *pair(8, 2), *pair(8, 2, 2), *pair(8, 2), *pair(8, 4), *pair(3, 2), *pair(4, 2, 2), *pair(4, 2),
             *pair(STEPS, 8), *pair(STEPS), *pair(8), *pair(1), *pair(STEPS, 8), *pair(STEPS, 8),
             *pair(STEPS), *pair(STEPS), *pair(STEPS, HEAD), *pair(STEPS, SEQ), *pair(HEAD), *pair(STEPS, HEAD),

time: 150 us -> 143 us (0.953)
  Pallas kernels: 147 us -> 140 us
    pallas_call x1, Pallas kernels: 147 us -> 140 us  [on_device(): pl.pallas_call(kernel, out_shape=(rows, rows, rows), in_specs=[anywhere]...]
where the time goes in v5:
time: 143 us
  Pallas kernels  140 us (98%)
  other arithmetic  1.94 us (1%)
    pallas_call x1, Pallas kernels, on_device(): pl.pallas_call(kernel, out_shape=(rows, rows, rows), in_specs=[anywhere]...  140 us

profile of v5, /device:TPU:6, one launch (start us, length us, event | category | flops | bytes accessed | tf_op | source)
XLA Modules:
  0.0 143.0 jit_solution(825134499590459712)
XLA Ops:
  0.6 140.4 %beam_decode.1 = (f32[16,4096]{1,0:T(8,128)}, f32[16,4096]{1,0:T(8,128)}, f32[16,4096]{1,0:T(8,128)}) custom-call(bf16[1024,256]{1,0:T(8,128)(2,1)} %enc.1, f32[1,4096]{1,0:T(1,128)} %bitcast.2, bf16[512,256]{1,0:T(8,128)(2,1)} %wk.1, bf16[512,256]{1,0:T(8,128)(2,1)} %wv.1, bf16[512,256]{1,0:T(8,128)(2,1)} %wq_in.1, bf16[256,512]{1,0:T(8,128)(2,1)} %wo_in.1, ...), custom_call_target="tpu_custom_call" | custom-call | tf_op jit(solution)/shard_map/beam_decode/pallas_call | solution.py:538
  141.1 1.9 %fusion = (f32[16,4096]{1,0:T(8,128)}, f32[16,4096]{1,0:T(8,128)}) fusion(f32[16,4096]{1,0:T(8,128)} %get-tuple-element.7, f32[16,4096]{1,0:T(8,128)} %get-tuple-element.6, f32[16,4096]{1,0:T(8,128)} %get-tuple-element.5), kind=kLoop, calls=%fused_computation | loop fusion | flops 131072 | bytes 1310720 | tf_op jit(solution)/shard_map/add | solution.py:595

commit v6 on v5

--- a/solution.py
+++ b/solution.py
@@ -57,11 +57,11 @@
     enc_gain, wq, wo, gain, first, tokens, out_pre, out_first, out_second,
     ebuf, nbuf, wbuf, kv,
     pre, part, picked, local_rows, full,
-    q_own, q_all, u_own, u_all, z_own, z_all, zz_own, zz_all, c_own, c_all, t_own, t_all, m_own, m_all, v_own, v_all,
+    q_own, q_all, w_own, w_all, u_own, u_all, z_own, z_all, zz_own, zz_all, c_own, c_all, t_own, t_all, m_own, m_all, v_own, v_all,
     p_own, p_all, f_own, f_all, l_all, g_all,
     own_sem, in_sem, out_sem, wz_ss, wz_rs, wy_ss, wy_rs, wh_ss, wh_rs, wc_ss, wc_rs, ez_ss, ez_rs, ex_ss, ex_rs, eh_ss, eh_rs,
     q_ss, q_rs, u_ss, u_rs, z_ss, z_rs, zz_ss, zz_rs, c_ss, c_rs, t_ss, t_rs, m_ss, m_rs, v_ss, v_rs,
-    p_ss, p_rs, f_ss, f_rs, l_ss, l_rs, g_ss, g_rs,
+    p_ss, p_rs, f_ss, f_rs, l_ss, l_rs, g_ss, g_rs, e_ss, e_rs,
 ):
     y, s, c, k, zl, x, b, r, n = place()
     up, down = {"src": lax.rem(y + 1, 4)}, {"src": lax.rem(y + 3, 4)}
@@ -260,20 +260,23 @@
             m = ring_peers[i]
             if t == 1:
                 send(z_own, z_all.at[n], z_ss.at[i], z_rs.at[n], ring(m))
-            send(q_own.at[t], q_all.at[t, n], q_ss.at[t, i], q_rs.at[t, n], ring(m))
+            mine, theirs = (w_own, w_all) if t == 1 else (q_own, q_all)
+            send(mine, theirs.at[n], q_ss.at[t, i], q_rs.at[t, n], ring(m))
 
     def query_swap(t):
         for i, m in enumerate(ring_peers):
             if t == 1:
                 wait_arrival(z_all.at[m], z_ss.at[i], z_rs.at[m], ring(m))
-            wait_arrival(q_all.at[t, m], q_ss.at[t, i], q_rs.at[t, m], ring(m))
+            wait_arrival((w_all if t == 1 else q_all).at[m], q_ss.at[t, i], q_rs.at[t, m], ring(m))
         if t == 1:
             squares = (z_all[0] + z_all[2]) + (z_all[4] + z_all[6])
             zz_own[...] = squares
             zz_all[k] = squares
             send(zz_own, zz_all.at[k], zz_ss.at[0], zz_rs.at[0], partner)
         for g in range(2):
-            both_g = (q_all[t, g] + q_all[t, g + 2]) + (q_all[t, g + 4] + q_all[t, g + 6])
+            source = w_all if t == 1 else q_all
+            each = [source[m].astype(jnp.float32) for m in range(g, 8, 2)]
+            both_g = (each[0] + each[1]) + (each[2] + each[3])
             u_all[t, k, g] = both_g
             u_own[t, g] = both_g
         send(u_own.at[t], u_all.at[t, k], u_ss.at[t], u_rs.at[t], partner)
@@ -326,8 +329,8 @@
     pre[...] = start
     mean = jnp.sum(start * start, axis=-1, keepdims=True) * (1.0 / 4096.0)
     picked[...] = start * lax.rsqrt(mean + 1e-06) * gain[...]
-    q_own[0] = jnp.dot(picked[:, feats].astype(jnp.bfloat16), wq[...], preferred_element_type=jnp.float32)
-    q_all[0, n] = q_own[0]
+    q_own[...] = jnp.dot(picked[:, feats].astype(jnp.bfloat16), wq[...], preferred_element_type=jnp.float32)
+    q_all[n] = q_own[...]
 
     z_step(1, 0)
     z_step(2, 0)
@@ -363,7 +366,6 @@
     query_out(0)
     y_last(1)
     y_last(2)
-    query_swap(0)
     y_relay(5)
     y_relay(6)
     y_cross(3)
@@ -378,8 +380,6 @@
     y_last(5)
     y_last(6)
     x_last(3)
-    y_cross(7)
-    y_last(7)
 
     @pl.loop(0, 8)
     def _(i):
@@ -395,6 +395,9 @@
             block = ebuf[f, at, :].astype(jnp.float32) * scale * enc_gain[:, cols]
             nbuf[at, cols] = block.astype(jnp.bfloat16)
 
+    y_cross(7)
+    y_last(7)
+    query_swap(0)
     wait_arrival(shard_both(other), wc_ss.at[0, 0], wc_rs.at[0, 0], partner)
     for q in range(1, 8):
         for j in range(4):
@@ -421,10 +424,11 @@
             scaled = rows * gain[:, feats]
             high = scaled.astype(jnp.bfloat16)
             low = (scaled - high.astype(jnp.float32)).astype(jnp.bfloat16)
-            q_own[1] = jnp.dot(high, wq[...], preferred_element_type=jnp.float32) + jnp.dot(
+            partial = jnp.dot(high, wq[...], preferred_element_type=jnp.float32) + jnp.dot(
                 low, wq[...], preferred_element_type=jnp.float32
             )
-            q_all[1, n] = q_own[1]
+            w_own[...] = partial.astype(jnp.bfloat16)
+            w_all[n] = w_own[...]
             query_out(1)
             query_swap(1)
             for i, p in enumerate(seq_peers):
@@ -503,13 +507,24 @@
         if t == 0:
             for i, p in enumerate(head_peers):
                 wait_arrival(l_all.at[p], l_ss.at[i], l_rs.at[p], {"head": p})
-    for i, p in enumerate(seq_peers):
-        wait_arrival(f_all.at[1, p], f_ss.at[1, i], f_rs.at[1, p], {"seq": p})
-    for i, p in enumerate(head_peers):
-        send(f_all.at[1], g_all.at[1, c], g_ss.at[1, i], g_rs.at[1, c], {"head": p})
+    z_hi = lax.div(s, 2)
+    slices = [lax.rem(z_hi + i, 4) for i in (0, 1, 3, 2)]
+    for i, z_from in enumerate(slices):
+        for core in (0, 1):
+            if i == 0:
+                continue
+            p = 2 * z_from + core
+            wait_arrival(f_all.at[1, p], f_ss.at[1, 0], f_rs.at[1, p], partner)
+        if i == 0:
+            wait_arrival(f_all.at[1, s + 1 - 2 * k], f_ss.at[1, 0], f_rs.at[1, s + 1 - 2 * k], partner)
+        two = pl.ds(2 * z_from, 2)
+        for h, p in enumerate(head_peers):
+            send(f_all.at[1, two], g_all.at[1, c, two], e_ss.at[i, h], e_rs.at[i, c], {"head": p})
     g_all[1, c] = f_all[1]
-    for i, p in enumerate(head_peers):
-        wait_arrival(g_all.at[1, p], g_ss.at[1, i], g_rs.at[1, p], {"head": p})
+    for i, z_from in enumerate(slices):
+        two = pl.ds(2 * z_from, 2)
+        for h, p in enumerate(head_peers):
+            wait_arrival(g_all.at[1, p, two], e_ss.at[i, h], e_rs.at[i, p], {"head": p})
     for i in range(8):
         for j in range(4):
             cols = slice(512 * i + 128 * j, 512 * i + 128 * j + 128)
@@ -559,8 +574,10 @@
             pltpu.VMEM((BEAMS, 4096), f32),
             pltpu.VMEM((BEAMS, 512), f32),
             pltpu.VMEM((BEAMS, 4096), f32),
-            pltpu.VMEM((STEPS, BEAMS, 256), f32),
-            pltpu.VMEM((STEPS, 8, BEAMS, 256), f32),
+            pltpu.VMEM((BEAMS, 256), f32),
+            pltpu.VMEM((8, BEAMS, 256), f32),
+            pltpu.VMEM((BEAMS, 256), bf16),
+            pltpu.VMEM((8, BEAMS, 256), bf16),
             pltpu.VMEM((STEPS, 2, BEAMS, 256), f32),
             pltpu.VMEM((STEPS, 2, 2, BEAMS, 256), f32),
             pltpu.VMEM((1, 128), f32),
@@ -584,7 +601,7 @@
             dma((3,)), dma((6,)), dma((3,)),
             *pair(8, 2), *pair(8, 2, 2), *pair(8, 2), *pair(8, 4), *pair(3, 2), *pair(4, 2, 2), *pair(4, 2),
             *pair(STEPS, 8), *pair(STEPS), *pair(8), *pair(1), *pair(STEPS, 8), *pair(STEPS, 8),
-            *pair(STEPS), *pair(STEPS), *pair(STEPS, HEAD), *pair(STEPS, SEQ), *pair(HEAD), *pair(STEPS, HEAD),
+            *pair(STEPS), *pair(STEPS), *pair(STEPS, HEAD), *pair(STEPS, SEQ), *pair(HEAD), *pair(STEPS, HEAD), *pair(4, HEAD),
         ],
         compiler_params=pltpu.CompilerParams(collective_id=1, has_side_effects=True),
         name="beam_decode",

time: 143 us -> 136 us (0.951)
  Pallas kernels: 140 us -> 132 us
    pallas_call x1, Pallas kernels: 140 us -> 132 us  [on_device(): pl.pallas_call(kernel, out_shape=(rows, rows, rows), in_specs=[anywhere]...]
where the time goes in v6:
time: 136 us; the launch traced here: 135 us
  Pallas kernels  132 us (97%)
  other arithmetic  1.94 us (1%)
    pallas_call x1, Pallas kernels, on_device(): pl.pallas_call(kernel, out_shape=(rows, rows, rows), in_specs=[anywhere]...  132 us

profile of v6, /device:TPU:6, one launch (start us, length us, event | category | flops | bytes accessed | tf_op | source)
XLA Modules:
  0.0 134.8 jit_solution(12615076680082891739)
XLA Ops:
  0.6 132.2 %beam_decode.1 = (f32[16,4096]{1,0:T(8,128)}, f32[16,4096]{1,0:T(8,128)}, f32[16,4096]{1,0:T(8,128)}) custom-call(bf16[1024,256]{1,0:T(8,128)(2,1)} %enc.1, f32[1,4096]{1,0:T(1,128)} %bitcast.2, bf16[512,256]{1,0:T(8,128)(2,1)} %wk.1, bf16[512,256]{1,0:T(8,128)(2,1)} %wv.1, bf16[512,256]{1,0:T(8,128)(2,1)} %wq_in.1, bf16[256,512]{1,0:T(8,128)(2,1)} %wo_in.1, ...), custom_call_target="tpu_custom_call" | custom-call | tf_op jit(solution)/shard_map/beam_decode/pallas_call | solution.py:553
  132.8 1.9 %fusion = (f32[16,4096]{1,0:T(8,128)}, f32[16,4096]{1,0:T(8,128)}) fusion(f32[16,4096]{1,0:T(8,128)} %get-tuple-element.7, f32[16,4096]{1,0:T(8,128)} %get-tuple-element.6, f32[16,4096]{1,0:T(8,128)} %get-tuple-element.5), kind=kLoop, calls=%fused_computation | loop fusion | flops 131072 | bytes 1310720 | tf_op jit(solution)/shard_map/add | solution.py:612

commit v7 on v6

--- a/solution.py
+++ b/solution.py
@@ -310,6 +310,12 @@
                 stats = jnp.where(lane == 8 * half + h, top[at:at + 8], stats)
                 stats = jnp.where(lane == 8 * half + 4 + h, total[at:at + 8], stats)
         return ctx.astype(jnp.bfloat16), stats
+
+    def project(g):
+        @pl.loop(0, 2)
+        def _(i):
+            at = 2 * g + i
+            kv[at] = jnp.dot(nbuf[...], wbuf[at], preferred_element_type=jnp.float32).astype(jnp.bfloat16)
 
     z_on(0, 0)
     z_on(0, 1)
@@ -398,14 +404,16 @@
     y_cross(7)
     y_last(7)
     query_swap(0)
-    wait_arrival(shard_both(other), wc_ss.at[0, 0], wc_rs.at[0, 0], partner)
-    for q in range(1, 8):
+
+    for q in (1, 2, 5, 6):
         for j in range(4):
             wait_arrival(both(q, j, other), wc_ss.at[q, j], wc_rs.at[q, j], partner)
-
-    @pl.loop(0, 4)
-    def _(i):
-        kv[i] = jnp.dot(nbuf[...], wbuf[i], preferred_element_type=jnp.float32).astype(jnp.bfloat16)
+    project(1 - r)
+    wait_arrival(shard_both(other), wc_ss.at[0, 0], wc_rs.at[0, 0], partner)
+    for q in (3, 4, 7):
+        for j in range(4):
+            wait_arrival(both(q, j, other), wc_ss.at[q, j], wc_rs.at[q, j], partner)
+    project(r)
 
     for t in range(STEPS):
         scale = None
@@ -431,11 +439,6 @@
             w_all[n] = w_own[...]
             query_out(1)
             query_swap(1)
-            for i, p in enumerate(seq_peers):
-                wait_arrival(f_all.at[0, p], f_ss.at[0, i], f_rs.at[0, p], {"seq": p})
-            for i, p in enumerate(head_peers):
-                send(f_all.at[0], g_all.at[0, c], g_ss.at[0, i], g_rs.at[0, c], {"head": p})
-            g_all[0, c] = f_all[0]
         query_in(t)
         if t == 1:
             table = lax.rsqrt(unfold(zz_all[0] + zz_all[1]) * (1.0 / 4096.0) + 1e-06)
@@ -451,6 +454,11 @@
         c_all[t, n] = c_own[t, 1]
         t_all[t, n] = t_own[t, 1]
         if t == 1:
+            for i, p in enumerate(seq_peers):
+                wait_arrival(f_all.at[0, p], f_ss.at[0, i], f_rs.at[0, p], {"seq": p})
+            for i, p in enumerate(head_peers):
+                send(f_all.at[0], g_all.at[0, c], g_ss.at[0, i], g_rs.at[0, c], {"head": p})
+            g_all[0, c] = f_all[0]
             for i, p in enumerate(head_peers):
                 wait_arrival(g_all.at[0, p], g_ss.at[0, i], g_rs.at[0, p], {"head": p})
             for i in range(8):

time: 136 us -> 137 us (level)
  Pallas kernels: 132 us -> 134 us
    pallas_call x1, Pallas kernels: 132 us -> 134 us  [on_device(): pl.pallas_call(kernel, out_shape=(rows, rows, rows), in_specs=[anywhere]...]
where the time goes in v7:
time: 137 us
  Pallas kernels  134 us (98%)
  other arithmetic  1.94 us (1%)
    pallas_call x1, Pallas kernels, on_device(): pl.pallas_call(kernel, out_shape=(rows, rows, rows), in_specs=[anywhere]...  134 us

profile of v7, /device:TPU:6, one launch (start us, length us, event | category | flops | bytes accessed | tf_op | source)
XLA Modules:
  0.0 136.6 jit_solution(16588413171846826934)
XLA Ops:
  0.6 134.0 %beam_decode.1 = (f32[16,4096]{1,0:T(8,128)}, f32[16,4096]{1,0:T(8,128)}, f32[16,4096]{1,0:T(8,128)}) custom-call(bf16[1024,256]{1,0:T(8,128)(2,1)} %enc.1, f32[1,4096]{1,0:T(1,128)} %bitcast.2, bf16[512,256]{1,0:T(8,128)(2,1)} %wk.1, bf16[512,256]{1,0:T(8,128)(2,1)} %wv.1, bf16[512,256]{1,0:T(8,128)(2,1)} %wq_in.1, bf16[256,512]{1,0:T(8,128)(2,1)} %wo_in.1, ...), custom_call_target="tpu_custom_call" | custom-call | tf_op jit(solution)/shard_map/beam_decode/pallas_call | solution.py:561
  134.7 1.9 %fusion = (f32[16,4096]{1,0:T(8,128)}, f32[16,4096]{1,0:T(8,128)}) fusion(f32[16,4096]{1,0:T(8,128)} %get-tuple-element.7, f32[16,4096]{1,0:T(8,128)} %get-tuple-element.6, f32[16,4096]{1,0:T(8,128)} %get-tuple-element.5), kind=kLoop, calls=%fused_computation | loop fusion | flops 131072 | bytes 1310720 | tf_op jit(solution)/shard_map/add | solution.py:620
